TPU v7x, 512 devices: a whole 4x8x8 slice. The times are simulated.
512 devices in a mesh: ctx: 64 (over y_hi, z, core), tp: 8 (over x, y_lo).
Axes of the slice: x: 4, y: 8 (y_hi: 4, y_lo: 2; y = y_hi * 2 + y_lo), z: 8, core: 2. Of those that a mesh axis runs over, the one named last changes fastest.
Arguments:
- q_new: bfloat16 [1024, 8192], P(('ctx', 'tp')), may hold values from -128 to 128
- kv_new: bfloat16 [2, 1024, 1024], P(None, 'ctx', 'tp'), may hold values from -4 to 4
- kv_cache: bfloat16 [2, 31744, 1024], P(None, 'ctx', 'tp'), may hold values from -4 to 4
- cache_lens: int32 [64], replicated, may hold values from 1 to 496, 15872 in all
- segment_ids: int32 [1024], replicated, may hold values from 0 to 63, never falling along the last dimension, each value on 1 to 32 neighbouring positions
Outputs:
- attn_out: bfloat16 [1024, 8192], P(('ctx', 'tp'))
- attn_lse: float32 [1024, 64], P('ctx', 'tp')
Inputs may be any that keep to these rules, and one draw needn't show every extreme that they name: The filled slots of shard c are its first cache_lens[c] slots; the lengths sum to 15872 and some shard is full. `segment_ids`: never falls along the turn; a segment holds at most 32 tokens, and some segment exactly 32.
All inputs are finite; a program needn't handle non-finite values.
Results may differ from a plain program's by a relative error of at most 0.0015.
Values may be sent and summed in bfloat16 or wider, within the bound.
No kernel may reach another device: no remote copies, remote signals or barrier semaphores. Data moves between devices by JAX's collectives and lax.ppermute only.
A program may use at most 64 MiB of HBM per device.

v0:
```python
import jax
import jax.numpy as jnp
from jax import lax
from jax.sharding import PartitionSpec as P


def shard_partial(queries, query_seg, keys_all, values_all, filled, key_seg, head_dim):
    rows = queries.shape[0]
    heads = queries.shape[1] // head_dim
    total = keys_all.shape[0]
    cache_count = total - key_seg.shape[0]
    flat = queries.reshape(rows * heads, head_dim)
    scores = lax.dot_general(
        flat, keys_all, (((1,), (1,)), ((), ())), preferred_element_type=jnp.float32
    ) * head_dim ** (-0.5)
    scores = scores.reshape(rows, heads, total)
    slot_rank = jnp.where(jnp.arange(cache_count) < filled, -1, 2**30).astype(jnp.int32)
    key_rank = jnp.concatenate([slot_rank, key_seg])
    visible = key_rank[None, None, :] <= query_seg[:, None, None]
    masked = jnp.where(visible, scores, -jnp.inf)
    peak = jnp.max(masked, axis=2)
    expo = jnp.exp(masked - peak[:, :, None])
    denom = jnp.sum(expo, axis=2)
    weights = expo.astype(jnp.bfloat16).reshape(rows * heads, total)
    mixed = jnp.dot(weights, values_all, preferred_element_type=jnp.float32)
    mixed = mixed.reshape(rows, heads, head_dim) / denom[:, :, None]
    return (mixed.reshape(rows, heads * head_dim), peak + jnp.log(denom))


def shards(q_new, kv_new, kv_cache, cache_lens, segment_ids):
    head_dim = kv_cache.shape[2]
    block = kv_new.shape[1]
    here = lax.axis_index("ctx")
    count = lax.axis_size("ctx")
    queries = lax.all_to_all(q_new, "tp", split_axis=1, concat_axis=0, tiled=True)
    heads = queries.shape[1] // head_dim
    keys_all = jnp.concatenate([kv_cache[0], kv_new[0]])
    values_all = jnp.concatenate([kv_cache[1], kv_new[1]])
    filled = cache_lens[here]
    key_seg = lax.dynamic_slice_in_dim(segment_ids, here * block, block, 0)
    total_rows = block * count
    init = (
        jnp.zeros((total_rows, heads * head_dim), jnp.float32),
        jnp.zeros((total_rows, heads), jnp.float32),
    )
    piece = lax.all_gather(queries, "ctx", axis=0, tiled=True)
    rows = piece.shape[0]
    width = 64

    def one_block(index, inner):
        outs, lses = inner
        offset = index * width
        part = lax.dynamic_slice_in_dim(piece, index * width, width, 0)
        part_seg = lax.dynamic_slice_in_dim(segment_ids, offset, width, 0)
        mixed, lse = shard_partial(part, part_seg, keys_all, values_all, filled, key_seg, head_dim)
        outs = lax.dynamic_update_slice_in_dim(outs, mixed, offset, 0)
        lses = lax.dynamic_update_slice_in_dim(lses, lse, offset, 0)
        return (outs, lses)

    partial_out, partial_lse = lax.fori_loop(0, rows // width, one_block, init)
    got_out, got_lse = (
        lax.all_to_all(
            partial_out.reshape(count, block, heads * head_dim),
            "ctx",
            split_axis=0,
            concat_axis=0,
            tiled=True,
        ),
        lax.all_to_all(
            partial_lse.reshape(count, block, heads), "ctx", split_axis=0, concat_axis=0, tiled=True
        ),
    )
    peak = jnp.max(got_lse, axis=0)
    scale = jnp.exp(got_lse - peak[None])
    denom = jnp.sum(scale, axis=0)
    numer = jnp.sum(got_out.reshape(count, block, heads, head_dim) * scale[:, :, :, None], axis=0)
    final = (numer / denom[:, :, None]).reshape(block, heads * head_dim)
    lse_out = peak + jnp.log(denom)
    attn_out = lax.all_to_all(
        final.astype(jnp.bfloat16), "tp", split_axis=0, concat_axis=1, tiled=True
    )
    return (attn_out, lse_out)


def solution(mesh):
    return jax.shard_map(
        shards,
        mesh=mesh,
        in_specs=(P(("ctx", "tp"), None), P(None, "ctx", "tp"), P(None, "ctx", "tp"), P(), P()),
        out_specs=(P(("ctx", "tp"), None), P("ctx", "tp")),
        check_vma=False,
    )
```

profile of v0, /device:TPU:272, one launch (start us, length us, event | category | flops | bytes accessed | tf_op | source)
XLA Modules:
  0.0 346.2 jit_solution(2459077010839411977)
XLA Ops:
  7.2 11.6 %all_to_all.45 = bf16[2,8,1024]{2,0,1:T(2,128)(2,1)S(1)} all-to-all(bf16[2,8,1024]{2,0,1:T(2,128)(2,1)} %bitcast.53), channel_id=1, replica_groups=mesh['ctx'=64,'tp'=8] {'tp'}, dimensions={1} | all-to-all | bytes 65536 | tf_op jit(solution)/shard_map/all_to_all | solution.py:35
  19.5 1.2 dynamic_slice.20
  22.2 1.0 slice_bitcast_fusion
  23.2 76.2 %all-gather.2.cloned.1.call-done = bf16[1024,1024]{1,0:T(8,128)(2,1)} async-done(((bf16[16,1024]{1,0:T(8,128)(2,1)}), bf16[1024,1024]{1,0:T(8,128)(2,1)}) %all-gather.2.cloned.1.call-update) | async-done | bytes 2097168 | tf_op jit(solution)/shard_map/all_gather | solution.py:46
  99.4 2.5 broadcast_in_dim.61
  102.0 74.2 %while.15 = (s32[]{:T(128)}, f32[1024,1024]{1,0:T(8,128)}, f32[1024,8]{1,0:T(8,128)S(1)}, s32[]{:T(128)}, s32[16]{0:T(128)S(1)}, /*index=5*/s32[1024]{0:T(1024)}...) while((s32[]{:T(128)}, f32[1024,1024]{1,0:T(8,128)}, ...), condition=%wide.region_3.4_spmd, body=%wide.region_0.3_spmd.sunk | while | flops 136152032 | bytes 5041031 | solution.py:60
  102.0 0.9 constant_dynamic-slice_fusion.2
  106.6 0.9 constant_dynamic-slice_fusion.2
  111.2 0.9 constant_dynamic-slice_fusion.2
  115.0 0.8 bitcast_dynamic-update-slice_fusion.2
  115.9 0.9 constant_dynamic-slice_fusion.2
  119.6 0.8 bitcast_dynamic-update-slice_fusion.2
  120.5 0.9 constant_dynamic-slice_fusion.2
  125.2 0.9 constant_dynamic-slice_fusion.2
  129.8 0.9 constant_dynamic-slice_fusion.2
  134.5 0.9 constant_dynamic-slice_fusion.2
  139.1 0.9 constant_dynamic-slice_fusion.2
  143.8 0.9 constant_dynamic-slice_fusion.2
  148.4 0.9 constant_dynamic-slice_fusion.2
  153.0 0.9 constant_dynamic-slice_fusion.2
  157.7 0.9 constant_dynamic-slice_fusion.2
  162.3 0.9 constant_dynamic-slice_fusion.2
  166.9 0.9 constant_dynamic-slice_fusion.2
  171.5 0.9 constant_dynamic-slice_fusion.2
  176.5 16.2 %all_to_all.46 = f32[64,1,128]{2,1,0:T(1,128)S(1)} all-to-all(f32[64,1,128]{2,1,0:T(1,128)S(1)} %reshape.108), channel_id=1, replica_groups=mesh['ctx'=64,'tp'=8] {'ctx'}, dimensions={0} | all-to-all | bytes 65536 | tf_op jit(solution)/shard_map/all_to_all | solution.py:69
  192.7 12.0 %all-to-all-start.1 = ((f32[64,16,1024]{2,1,0:T(8,128)}), f32[64,16,1024]{2,1,0:T(8,128)}, u32[]{:S(2)}, u32[]{:S(2)}) async-start(f32[64,16,1024]{2,1,0:T(8,128)} %bitcast.46), calls=%async_computation.1 | async-start | bytes 8388608 | tf_op jit(solution)/shard_map/all_to_all | solution.py:62
  206.9 2.6 mul.30
  209.4 4.9 %mul.31 = f32[64,16,1024]{2,1,0:T(8,128)} reshape(f32[64,16,8,128]{3,2,1,0:T(8,128)} %mul.30) | data formatting | bytes 8388608 | tf_op jit(solution)/shard_map/mul | solution.py:76
  214.5 109.1 %all-to-all-done.1 = f32[64,16,1024]{2,1,0:T(8,128)} async-done(((f32[64,16,1024]{2,1,0:T(8,128)}), f32[64,16,1024]{2,1,0:T(8,128)}, u32[]{:S(2)}, u32[]{:S(2)}) %all-to-all-start.1) | async-done | bytes 4194336 | tf_op jit(solution)/shard_map/all_to_all | solution.py:62
  323.6 4.0 %multiply_reduce_fusion = f32[16,1024]{1,0:T(8,128)S(1)} fusion(f32[64,16,1024]{2,1,0:T(8,128)} %all-to-all-done.1, f32[64,16,1024]{2,1,0:T(8,128)} %mul.31), kind=kLoop, calls=%fused_computation.16 | loop fusion | flops 2080768 | bytes 8454144 | tf_op jit(solution)/shard_map/reduce_sum | solution.py:76
  328.2 4.3 %all-to-all-start.3 = ((bf16[8,2,1024]{2,1,0:T(2,128)(2,1)}), bf16[8,2,1024]{2,1,0:T(2,128)(2,1)S(1)}, u32[]{:S(2)}, u32[]{:S(2)}) async-start(bf16[8,2,1024]{2,1,0:T(2,128)(2,1)} %divide_convert_fusion), calls=%async_computation.3 | async-start | bytes 65536 | tf_op jit(solution)/shard_map/all_to_all | solution.py:79
  333.2 5.6 %all-to-all-done.3 = bf16[8,2,1024]{2,1,0:T(2,128)(2,1)S(1)} async-done(((bf16[8,2,1024]{2,1,0:T(2,128)(2,1)}), bf16[8,2,1024]{2,1,0:T(2,128)(2,1)S(1)}, u32[]{:S(2)}, u32[]{:S(2)}) %all-to-all-start.3) | async-done | bytes 32800 | tf_op jit(solution)/shard_map/all_to_all | solution.py:79
  (214 shorter events, 63.5 us)
Async XLA Ops:
  7.2 92.2 %all-gather.2.cloned.1.call-start = ((), (), s32[]{:S(2)}) async-start(), calls=%async_computation.4 | async-start | bytes 2129920 | tf_op jit(solution)/shard_map/all_gather | solution.py:46
  192.7 130.9 %all-to-all-start.1 = ((f32[64,16,1024]{2,1,0:T(8,128)}), f32[64,16,1024]{2,1,0:T(8,128)}, u32[]{:S(2)}, u32[]{:S(2)}) async-start(f32[64,16,1024]{2,1,0:T(8,128)} %bitcast.46), calls=%async_computation.1 | async-start | bytes 8388608 | tf_op jit(solution)/shard_map/all_to_all | solution.py:62
  328.2 10.5 %all-to-all-start.3 = ((bf16[8,2,1024]{2,1,0:T(2,128)(2,1)}), bf16[8,2,1024]{2,1,0:T(2,128)(2,1)S(1)}, u32[]{:S(2)}, u32[]{:S(2)}) async-start(bf16[8,2,1024]{2,1,0:T(2,128)(2,1)} %divide_convert_fusion), calls=%async_computation.3 | async-start | bytes 65536 | tf_op jit(solution)/shard_map/all_to_all | solution.py:79
Sparse Core Ops, SparseCore 0:
  19.6 79.7 all-gather.1
where the time goes:
time: 348 us; the launch traced here: 346 us
  waiting for transfers between devices  191 us (55%)
  local copies, waits for them, and re-layouts  60.1 us (17%)
  blocking collectives  27.8 us (8%)
  other arithmetic  23.3 us (7%)
  starting transfers between devices  16.3 us (5%)
  between operations  14.1 us (4%)
  matrix products  12.4 us (4%)
    all_to_all x1, waiting for transfers between devices, shards(): lax.all_to_all(partial_out.reshape(count, block, heads * head_dim), 'ctx'...  109 us
    all_gather x1, waiting for transfers between devices, shards(): piece = lax.all_gather(queries, 'ctx', axis=0, tiled=True)  76.2 us
    all_to_all x1, blocking collectives, shards(): lax.all_to_all(partial_lse.reshape(count, block, heads), 'ctx', split_axi...  16.2 us
    dynamic_slice x16, local copies, waits for them, and re-layouts, one_block(): part = lax.dynamic_slice_in_dim(piece, index * width, width, 0)  14.7 us
    dynamic_update_slice x16, local copies, waits for them, and re-layouts, one_block(): outs = lax.dynamic_update_slice_in_dim(outs, mixed, offset, 0)  12.2 us
    dynamic_slice x16, local copies, waits for them, and re-layouts, one_block(): part_seg = lax.dynamic_slice_in_dim(segment_ids, offset, width, 0)  12.2 us
    all_to_all x1, starting transfers between devices, shards(): lax.all_to_all(partial_out.reshape(count, block, heads * head_dim), 'ctx'...  12 us
    all_to_all x1, blocking collectives, shards(): lax.all_to_all(q_new, 'tp', split_axis=1, concat_axis=0, tiled=True)  11.6 us
  transfers between devices with their start and end apart: 3, of which 3 were waited for; matrix products, arithmetic and copies ran while one was open for 4% of the time, Pallas kernels for 0%

commit v1 on v0

v1 whole, which is shorter than its diff:
```python
import functools
import math

import jax
import jax.numpy as jnp
from jax import lax
from jax.experimental import pallas as pl
from jax.experimental.pallas import tpu as pltpu
from jax.sharding import Mesh
from jax.sharding import PartitionSpec as P

HEAD = 128
NEG = float("-inf")
CTX = ("yh", "z", "core")
TP = ("x", "yl")
ROUTE = ("z", "x", "yl")


def prep_kernel(lens_ref, ids_ref, place_ref, filled_ref, kseg_ref, qseg_ref):
    yh, z, core = place_ref[0], place_ref[1], place_ref[2]
    row = lax.broadcasted_iota(jnp.int32, (16, 256), 0)
    token = lax.broadcasted_iota(jnp.int32, (8, 128), 1) // 8
    which = lax.broadcasted_iota(jnp.int32, (8, 128), 0)
    filled = jnp.zeros((8, 128), jnp.int32)
    for j in range(8):
        shard = ((yh + 4 - j // 2) % 4) * 16 + z * 2 + (core + j % 2) % 2
        filled = jnp.where(which == j, lens_ref[shard], filled)
        seg = jnp.zeros((16, 256), jnp.int32)
        for i in range(16):
            seg = jnp.where(row == i, ids_ref[shard * 16 + i], seg)
        kseg_ref[j] = seg
    filled_ref[...] = filled
    for zz in range(8):
        first = (yh * 16 + zz * 2 + core) * 16
        seg = jnp.zeros((8, 128), jnp.int32)
        for i in range(16):
            seg = jnp.where(token == i, ids_ref[first + i], seg)
        qseg_ref[:, zz * 128 : (zz + 1) * 128] = seg


def prep(lens, ids, place):
    smem = pl.BlockSpec(memory_space=pltpu.SMEM)
    vmem = pl.BlockSpec(memory_space=pltpu.VMEM)
    return pl.pallas_call(
        prep_kernel,
        out_shape=(
            jax.ShapeDtypeStruct((8, 128), jnp.int32),
            jax.ShapeDtypeStruct((8, 16, 256), jnp.int32),
            jax.ShapeDtypeStruct((8, 1024), jnp.int32),
        ),
        in_specs=[smem, smem, smem],
        out_specs=(vmem, vmem, vmem),
        name="prep",
    )(lens, ids, place)


def attend_kernel(shards, has_state, final, *refs):
    q_ref, filled_ref, kseg_ref, qseg_ref = refs[:4]
    chunk_refs = refs[4 : 4 + len(shards)]
    rest = refs[4 + len(shards) :]
    state_ref = rest[0] if has_state else None
    out_ref = rest[-1]
    rows = q_ref.shape[0]
    total = chunk_refs[0].shape[1]
    cache = total - 16
    tile = 256
    scale = HEAD**-0.5
    factor = scale * math.log2(math.e)
    slot = lax.broadcasted_iota(jnp.int32, (cache, 128), 0)
    for part in range(rows // tile):
        cols = slice(part * tile, (part + 1) * tile)
        q = q_ref[cols, :]
        qseg = qseg_ref[0:1, cols]
        if has_state:
            acc = state_ref[0:HEAD, cols]
            peak = state_ref[HEAD : HEAD + 1, cols]
            denom = state_ref[HEAD + 1 : HEAD + 2, cols]
        else:
            acc = peak = denom = None
        for which, j in enumerate(shards):
            keys = chunk_refs[which][0]
            values = chunk_refs[which][1]
            s = lax.dot_general(keys, q, (((1,), (1,)), ((), ())), preferred_element_type=jnp.float32)
            bias = jnp.where(slot < filled_ref[j : j + 1, :], 0.0, NEG).astype(jnp.float32)
            old = s[:cache] + jnp.concatenate([bias, bias], axis=1)
            new = jnp.where(kseg_ref[j] <= qseg, s[cache:], NEG)
            m = jnp.maximum(jnp.max(old, axis=0, keepdims=True), jnp.max(new, axis=0, keepdims=True))
            old = jnp.exp2((old - m) * factor)
            new = jnp.exp2((new - m) * factor)
            l = jnp.sum(old, axis=0, keepdims=True) + jnp.sum(new, axis=0, keepdims=True)
            w = jnp.concatenate([old.astype(jnp.bfloat16), new.astype(jnp.bfloat16)], axis=0)
            o = lax.dot_general(values, w, (((0,), (0,)), ((), ())), preferred_element_type=jnp.float32)
            if acc is None:
                acc, peak, denom = o, m, l
            else:
                top = jnp.maximum(peak, m)
                keep = jnp.exp2((peak - top) * factor)
                fresh = jnp.exp2((m - top) * factor)
                acc = acc * keep + o * fresh
                denom = denom * keep + l * fresh
                peak = top
        if not final:
            out_ref[0:HEAD, cols] = acc
            out_ref[HEAD : HEAD + 1, cols] = peak
            out_ref[HEAD + 1 : HEAD + 2, cols] = denom
        else:
            acc = acc / denom
            lse = peak * scale + jnp.log(denom)
            for half in range(tile // 128):
                block = acc[:, half * 128 : (half + 1) * 128].T
                line = lse[:, half * 128 : (half + 1) * 128]
                for t in range(8):
                    at = ((part * (tile // 128) + half) * 8 + t) * 17
                    out_ref[at : at + 16, :] = block[t * 16 : (t + 1) * 16, :]
                    out_ref[at + 16 : at + 17, :] = line


def attend(shards, q, prepared, chunks, state=None, final=False):
    vmem = pl.BlockSpec(memory_space=pltpu.VMEM)
    operands = [q, *prepared, *chunks]
    aliases = {}
    shape = (1088, 128) if final else (HEAD + 8, q.shape[0])
    if state is not None:
        if not final:
            aliases = {len(operands): 0}
        operands.append(state)
    work = len(shards) * q.shape[0] * chunks[0].shape[1]
    return pl.pallas_call(
        functools.partial(attend_kernel, tuple(shards), state is not None, final),
        out_shape=jax.ShapeDtypeStruct(shape, jnp.float32),
        in_specs=[vmem] * len(operands),
        out_specs=vmem,
        input_output_aliases=aliases,
        cost_estimate=pl.CostEstimate(flops=4 * HEAD * work, transcendentals=work, bytes_accessed=1 << 20),
        compiler_params=pltpu.CompilerParams(vmem_limit_bytes=32 << 20),
        name="attend",
    )(*operands)


def combine_kernel(place_ref, got_ref, out_ref, lse_ref, turned_ref, line_ref):
    me = place_ref[3]
    lse = got_ref[pl.ds(16, 64, stride=17), :].reshape(8, 8, 128)
    peak = jnp.max(lse, axis=0)
    w = jnp.exp(lse - peak[None])
    denom = jnp.sum(w, axis=0)
    w = (w / denom[None]).reshape(64, 128)
    turned_ref[...] = jnp.concatenate([w, w], axis=0).T
    line_ref[...] = peak + jnp.log(denom)
    mine = turned_ref[pl.ds(pl.multiple_of(me * 16, 16), 16), :]
    for g in range(8):
        acc = None
        for z in range(8):
            at = z * 8 + g
            term = got_ref[at * 17 : at * 17 + 16, :] * mine[:, at : at + 1]
            acc = term if acc is None else acc + term
        acc = acc.astype(jnp.bfloat16)
        out_ref[0, g * 8 : (g + 1) * 8, :] = acc[:8]
        out_ref[1, g * 8 : (g + 1) * 8, :] = acc[8:]
    line = jnp.broadcast_to(line_ref[pl.ds(me, 1), :], (16, 128))
    row = lax.broadcasted_iota(jnp.int32, (16, 128), 0)
    table = line
    for i in range(1, 16):
        table = jnp.where(row == i, pltpu.roll(line, 128 - 8 * i, 1), table)
    lse_ref[...] = table[:, :8]


def combine(place, got):
    smem = pl.BlockSpec(memory_space=pltpu.SMEM)
    vmem = pl.BlockSpec(memory_space=pltpu.VMEM)
    return pl.pallas_call(
        combine_kernel,
        out_shape=(
            jax.ShapeDtypeStruct((2, 64, 128), jnp.bfloat16),
            jax.ShapeDtypeStruct((16, 8), jnp.float32),
        ),
        in_specs=[smem, vmem],
        out_specs=(vmem, vmem),
        scratch_shapes=[pltpu.VMEM((128, 128), jnp.float32), pltpu.VMEM((8, 128), jnp.float32)],
        name="combine",
    )(place, got)


def shards_program(q_new, kv_new, kv_cache, cache_lens, segment_ids):
    place = jnp.stack(
        [lax.axis_index("yh"), lax.axis_index("z"), lax.axis_index("core"), lax.axis_index(TP)]
    ).astype(jnp.int32)
    across = [(0, 1), (1, 0)]

    def shift(x, by):
        return lax.ppermute(x, "yh", [(i, (i + by) % 4) for i in range(4)])

    own = jnp.concatenate([kv_cache, kv_new], axis=1)
    one = shift(own, 1)
    three = shift(own, 3)
    two = shift(own, 2)
    q = q_new.reshape(2, 8, 8, HEAD).transpose(1, 0, 2, 3).reshape(1, 8, 16, HEAD)
    q = jnp.broadcast_to(q, (8, 8, 16, HEAD)).reshape(64, 16, HEAD)
    q = lax.all_to_all(q, ROUTE, split_axis=0, concat_axis=0, tiled=True).reshape(1024, HEAD)
    prepared = prep(cache_lens, segment_ids, place)
    own_x = lax.ppermute(own, "core", across)
    state = attend([0, 1], q, prepared, [own, own_x])
    one_x = lax.ppermute(one, "core", across)
    state = attend([2, 3], q, prepared, [one, one_x], state)
    three_x = lax.ppermute(three, "core", across)
    state = attend([6, 7], q, prepared, [three, three_x], state)
    two_x = lax.ppermute(two, "core", across)
    state = attend([4], q, prepared, [two], state)
    sent = attend([5], q, prepared, [two_x], state, final=True)
    got = lax.all_to_all(sent.reshape(64, 1, 2176), ROUTE, split_axis=0, concat_axis=0, tiled=True)
    out, lse = combine(place, got.reshape(1088, HEAD))
    return out.reshape(2, 8192), lse


def solution(mesh):
    fine = Mesh(mesh.devices.reshape(4, 8, 2, 4, 2), CTX + TP)
    rows = P(CTX + TP, None)
    kv = P(None, CTX, TP)
    return jax.shard_map(
        shards_program,
        mesh=fine,
        in_specs=(rows, kv, kv, P(), P()),
        out_specs=(rows, P(CTX, TP)),
        check_vma=False,
    )
```

time: 348 us -> 107 us (0.31)
  the two profiles are of different devices: /device:TPU:272 before, /device:TPU:16 now
where the time goes in v1:
time: 107 us
  starting transfers between devices  34.8 us (33%)
  blocking collectives  28.6 us (27%)
  Pallas kernels  17.7 us (17%)
  waiting for transfers between devices  17.5 us (16%)
  local copies, waits for them, and re-layouts  6.61 us (6%)
    all_to_all x1, blocking collectives, shards_program(): lax.all_to_all(sent.reshape(64, 1, 2176), ROUTE, split_axis=0, concat_axi...  28.6 us
    ppermute x3, waiting for transfers between devices, shift(): return lax.ppermute(x, 'yh', [(i, (i + by) % 4) for i in range(4)])  17.5 us
    all_to_all x1, starting transfers between devices, shards_program(): lax.all_to_all(q, ROUTE, split_axis=0, concat_axis=0, tiled=True)  14.9 us
    pallas_call x5, Pallas kernels, attend(): pl.pallas_call(functools.partial(attend_kernel, tuple(shards), state is n...  14 us
    ppermute x3, starting transfers between devices, shift(): return lax.ppermute(x, 'yh', [(i, (i + by) % 4) for i in range(4)])  11.8 us
    unnamed x15, local copies, waits for them, and re-layouts  5.11 us
    ppermute x1, starting transfers between devices, shards_program(): two_x = lax.ppermute(two, 'core', across)  2.41 us
  transfers between devices with their start and end apart: 8, of which 2 were waited for; matrix products, arithmetic and copies ran while one was open for 1% of the time, Pallas kernels for 13%

profile of v1, /device:TPU:16, one launch (start us, length us, event | category | flops | bytes accessed | tf_op | source)
XLA Modules:
  0.0 106.6 jit_solution(17161960810774544293)
XLA Ops:
  0.6 0.8 copy_bitcast_fusion.1
  1.4 0.7 broadcast_in_dim.8
  2.1 14.9 %all-to-all-start = ((bf16[64,16,128]{2,1,0:T(8,128)(2,1)}), bf16[64,16,128]{2,1,0:T(8,128)(2,1)S(1)}, u32[]{:S(2)}, u32[]{:S(2)}) async-start(bf16[64,16,128]{2,1,0:T(8,128)(2,1)} %bitcast.6), calls=%async_computation | async-start | bytes 524288 | tf_op jit(solution)/shard_map/all_to_all | solution.py:198
  17.1 0.0 copy-start.5
  17.1 0.7 copy-done.5
  17.8 4.8 %collective-permute-start.4 = (bf16[2,512,128]{2,1,0:T(8,128)(2,1)S(1)}, bf16[2,512,128]{2,1,0:T(8,128)(2,1)S(1)}, u32[]{:S(2)}, u32[]{:S(2)}) collective-permute-start(bf16[2,512,128]{2,1,0:T(8,128)(2,1)S(1)} %constant_dynamic-update-slice_fusion.refs_4_), channel_id=1, source_target_pairs={{0,128},{128,256},{256,384},{384,0},{1,129},{129,257},{257,385},{3... | collective-permute-start | bytes 786440 | tf_op jit(solution)/shard_map/ppermute | solution.py:190
  22.6 1.9 %collective-permute-start.2 = (bf16[2,512,128]{2,1,0:T(8,128)(2,1)S(1)}, bf16[2,512,128]{2,1,0:T(8,128)(2,1)S(1)}, u32[]{:S(2)}, u32[]{:S(2)}) collective-permute-start(bf16[2,512,128]{2,1,0:T(8,128)(2,1)S(1)} %constant_dynamic-update-slice_fusion.refs_4_), channel_id=1, source_target_pairs={{0,384},{128,0},{256,128},{384,256},{1,385},{129,1},{257,129},{385... | collective-permute-start | bytes 786440 | tf_op jit(solution)/shard_map/ppermute | solution.py:190
  24.5 5.0 %collective-permute-start = (bf16[2,512,128]{2,1,0:T(8,128)(2,1)S(1)}, bf16[2,512,128]{2,1,0:T(8,128)(2,1)S(1)}, u32[]{:S(2)}, u32[]{:S(2)}) collective-permute-start(bf16[2,512,128]{2,1,0:T(8,128)(2,1)S(1)} %constant_dynamic-update-slice_fusion.refs_4_), channel_id=1, source_target_pairs={{0,256},{128,384},{256,0},{384,128},{1,257},{129,385},{257,1},{385... | collective-permute-start | bytes 786440 | tf_op jit(solution)/shard_map/ppermute | solution.py:190
  29.6 1.9 %collective-permute-start.6 = (bf16[2,512,128]{2,1,0:T(8,128)(2,1)S(1)}, bf16[2,512,128]{2,1,0:T(8,128)(2,1)S(1)}, u32[]{:S(2)}, u32[]{:S(2)}) collective-permute-start(bf16[2,512,128]{2,1,0:T(8,128)(2,1)S(1)} %constant_dynamic-update-slice_fusion.refs_4_), channel_id=1, source_target_pairs={{0,8},{8,0},{1,9},{9,1},{2,10},{10,2},{3,11},{11,3},{4,12},{12,4},... | collective-permute-start | bytes 786440 | tf_op jit(solution)/shard_map/ppermute | solution.py:200
  31.5 2.7 %collective-permute-done.4.refs_4_ = bf16[2,512,128]{2,1,0:T(8,128)(2,1)S(1)} collective-permute-done((bf16[2,512,128]{2,1,0:T(8,128)(2,1)S(1)}, bf16[2,512,128]{2,1,0:T(8,128)(2,1)S(1)}, u32[]{:S(2)}, u32[]{:S(2)}) %collective-permute-start.4) | collective-permute-done | bytes 262176 | tf_op jit(solution)/shard_map/ppermute | solution.py:190
  34.2 1.9 %collective-permute-start.5 = (bf16[2,512,128]{2,1,0:T(8,128)(2,1)S(1)}, bf16[2,512,128]{2,1,0:T(8,128)(2,1)S(1)}, u32[]{:S(2)}, u32[]{:S(2)}) collective-permute-start(bf16[2,512,128]{2,1,0:T(8,128)(2,1)S(1)} %collective-permute-done.4.refs_4_), channel_id=1, source_target_pairs={{0,8},{8,0},{1,9},{9,1},{2,10},{10,2},{3,11},{11,3},{4,12},{12,4},... | collective-permute-start | bytes 786440 | tf_op jit(solution)/shard_map/ppermute | solution.py:202
  36.1 14.8 %collective-permute-done.2.refs_4_ = bf16[2,512,128]{2,1,0:T(8,128)(2,1)S(1)} collective-permute-done((bf16[2,512,128]{2,1,0:T(8,128)(2,1)S(1)}, bf16[2,512,128]{2,1,0:T(8,128)(2,1)S(1)}, u32[]{:S(2)}, u32[]{:S(2)}) %collective-permute-start.2) | collective-permute-done | bytes 262176 | tf_op jit(solution)/shard_map/ppermute | solution.py:190
  50.9 1.9 %collective-permute-start.3 = (bf16[2,512,128]{2,1,0:T(8,128)(2,1)S(1)}, bf16[2,512,128]{2,1,0:T(8,128)(2,1)S(1)}, u32[]{:S(2)}, u32[]{:S(2)}) collective-permute-start(bf16[2,512,128]{2,1,0:T(8,128)(2,1)S(1)} %collective-permute-done.2.refs_4_), channel_id=1, source_target_pairs={{0,8},{8,0},{1,9},{9,1},{2,10},{10,2},{3,11},{11,3},{4,12},{12,4},... | collective-permute-start | bytes 786440 | tf_op jit(solution)/shard_map/ppermute | solution.py:204
  52.9 0.0 collective-permute-done.refs_4_
  52.9 2.4 %collective-permute-start.1 = (bf16[2,512,128]{2,1,0:T(8,128)(2,1)S(1)}, bf16[2,512,128]{2,1,0:T(8,128)(2,1)S(1)}, u32[]{:S(2)}, u32[]{:S(2)}) collective-permute-start(bf16[2,512,128]{2,1,0:T(8,128)(2,1)S(1)} %collective-permute-done.refs_4_), channel_id=1, source_target_pairs={{0,8},{8,0},{1,9},{9,1},{2,10},{10,2},{3,11},{11,3},{4,12},{12,4},... | collective-permute-start | bytes 786440 | tf_op jit(solution)/shard_map/ppermute | solution.py:206
  55.3 0.6 pad_add_fusion.place_ref
  55.9 1.6 %prep.1 = (s32[8,128]{1,0:T(8,128)}, s32[8,16,256]{2,1,0:T(8,128)}, s32[8,1024]{1,0:T(8,128)}) custom-call(s32[64]{0:T(128)} %lens_ref.1, s32[1024]{0:T(1024)} %ids_ref.1, s32[4]{0:T(128)} %pad_add_fusion.place_ref), custom_call_target="tpu_custom_call" | custom-call | tf_op jit(solution)/shard_map/prep/pallas_call | solution.py:44
  57.4 0.0 collective-permute-done.6.refs_5_
  57.4 0.0 all-to-all-done
  57.4 0.7 copy-done.2
  58.1 0.9 copy-done
  59.0 0.8 copy-done.1
  59.8 3.4 %attend.5.refs_6_ = f32[136,1024]{1,0:T(8,128)S(1)} custom-call(bf16[1024,128]{1,0:T(8,128)(2,1)S(1)} %bitcast.22, s32[8,128]{1,0:T(8,128)S(1)} %copy-done.2, s32[8,16,256]{2,1,0:T(8,128)S(1)} %copy-done, s32[8,1024]{1,0:T(8,128)S(1)} %copy-done.1, bf16[2,512,128]{2,1,0:T(8,128)(2,1)S(1)} %constant_dynamic-update-slice_fusion.refs_4_, ...), custom_call_target="tpu_custom_call" | custom-call | flops 536870912 | bytes 1048576 | tf_op jit(solution)/shard_map/attend/pallas_call | solution.py:128
  63.2 0.0 collective-permute-done.5.refs_5_
  63.2 3.4 %attend.6.refs_6_ = f32[136,1024]{1,0:T(8,128)S(1)} custom-call(bf16[1024,128]{1,0:T(8,128)(2,1)S(1)} %bitcast.23, s32[8,128]{1,0:T(8,128)S(1)} %copy-done.2, s32[8,16,256]{2,1,0:T(8,128)S(1)} %copy-done, s32[8,1024]{1,0:T(8,128)S(1)} %copy-done.1, bf16[2,512,128]{2,1,0:T(8,128)(2,1)S(1)} %collective-permute-done.4.refs_4_, ...), custom_call_target="tpu_custom_call", output_to_operand_aliasing={{}: (6, {})} | custom-call | flops 536870912 | bytes 1048576 | tf_op jit(solution)/shard_map/attend/pallas_call | solution.py:128
  66.7 3.4 %attend.7.refs_5_ = f32[136,1024]{1,0:T(8,128)S(1)} custom-call(bf16[1024,128]{1,0:T(8,128)(2,1)S(1)} %bitcast.24, s32[8,128]{1,0:T(8,128)S(1)} %copy-done.2, s32[8,16,256]{2,1,0:T(8,128)S(1)} %copy-done, s32[8,1024]{1,0:T(8,128)S(1)} %copy-done.1, bf16[2,512,128]{2,1,0:T(8,128)(2,1)S(1)} %collective-permute-done.2.refs_4_, ...), custom_call_target="tpu_custom_call", output_to_operand_aliasing={{}: (6, {})} | custom-call | flops 536870912 | bytes 1048576 | tf_op jit(solution)/shard_map/attend/pallas_call | solution.py:128
  70.1 1.9 %attend.8.refs_5_ = f32[136,1024]{1,0:T(8,128)S(1)} custom-call(bf16[1024,128]{1,0:T(8,128)(2,1)S(1)} %bitcast.25, s32[8,128]{1,0:T(8,128)S(1)} %copy-done.2, s32[8,16,256]{2,1,0:T(8,128)S(1)} %copy-done, s32[8,1024]{1,0:T(8,128)S(1)} %copy-done.1, bf16[2,512,128]{2,1,0:T(8,128)(2,1)S(1)} %collective-permute-done.refs_4_, ...), custom_call_target="tpu_custom_call", output_to_operand_aliasing={{}: (5, {})} | custom-call | flops 268435456 | bytes 1048576 | tf_op jit(solution)/shard_map/attend/pallas_call | solution.py:128
  72.0 1.8 %attend.9 = f32[1088,128]{1,0:T(8,128)S(1)} custom-call(bf16[1024,128]{1,0:T(8,128)(2,1)S(1)} %bitcast.26, s32[8,128]{1,0:T(8,128)S(1)} %copy-done.2, s32[8,16,256]{2,1,0:T(8,128)S(1)} %copy-done, s32[8,1024]{1,0:T(8,128)S(1)} %copy-done.1, bf16[2,512,128]{2,1,0:T(8,128)(2,1)S(1)} %collective-permute-done.1.refs_4_, f32[136,1024]{1,0:T(8,128)S(1)} %attend.8.refs_5_), custom_call_target="tpu_custom_call" | custom-call | flops 268435456 | bytes 1048576 | tf_op jit(solution)/shard_map/attend/pallas_call | solution.py:128
  73.8 28.6 %all_to_all.10 = f32[64,1,2176]{2,1,0:T(1,128)} all-to-all(f32[64,1,2176]{2,1,0:T(1,128)S(1)} %bitcast.27), channel_id=1, replica_groups=mesh['yh'=4,'z'=8,'core'=2,'x'=4,'yl'=2] {'z','x','yl'}, dimensions={0} | all-to-all | bytes 1114112 | tf_op jit(solution)/shard_map/all_to_all | solution.py:209
  102.4 2.1 %combine.1 = (bf16[2,64,128]{2,1,0:T(8,128)(2,1)}, f32[16,8]{1,0:T(8,128)}) custom-call(s32[4]{0:T(128)} %pad_add_fusion.place_ref, f32[1088,128]{1,0:T(8,128)} %bitcast.28), custom_call_target="tpu_custom_call" | custom-call | tf_op jit(solution)/shard_map/combine/pallas_call | solution.py:170
  104.5 1.4 %copy.23 = bf16[1,2,64,128]{3,1,2,0:T(2,128)(2,1)} copy(bf16[1,2,64,128]{3,2,1,0:T(8,128)(2,1)} %bitcast.31) | data formatting | bytes 65536
  105.9 0.7 copy.16
  (11 shorter events, 0.0 us)
Async XLA Ops:
  2.1 14.9 %copy-start.3 = (bf16[2,496,128]{2,1,0:T(8,128)(2,1)S(1)}, bf16[2,496,128]{2,1,0:T(8,128)(2,1)}, u32[]{:S(2)}) copy-start(bf16[2,496,128]{2,1,0:T(8,128)(2,1)} %param.7) | copy-start | bytes 761860
  2.1 55.3 %all-to-all-start = ((bf16[64,16,128]{2,1,0:T(8,128)(2,1)}), bf16[64,16,128]{2,1,0:T(8,128)(2,1)S(1)}, u32[]{:S(2)}, u32[]{:S(2)}) async-start(bf16[64,16,128]{2,1,0:T(8,128)(2,1)} %bitcast.6), calls=%async_computation | async-start | bytes 524288 | tf_op jit(solution)/shard_map/all_to_all | solution.py:198
  17.1 0.7 copy-start.5
  17.8 16.5 %collective-permute-start.4 = (bf16[2,512,128]{2,1,0:T(8,128)(2,1)S(1)}, bf16[2,512,128]{2,1,0:T(8,128)(2,1)S(1)}, u32[]{:S(2)}, u32[]{:S(2)}) collective-permute-start(bf16[2,512,128]{2,1,0:T(8,128)(2,1)S(1)} %constant_dynamic-update-slice_fusion.refs_4_), channel_id=1, source_target_pairs={{0,128},{128,256},{256,384},{384,0},{1,129},{129,257},{257,385},{3... | collective-permute-start | bytes 786440 | tf_op jit(solution)/shard_map/ppermute | solution.py:190
  22.6 28.3 %collective-permute-start.2 = (bf16[2,512,128]{2,1,0:T(8,128)(2,1)S(1)}, bf16[2,512,128]{2,1,0:T(8,128)(2,1)S(1)}, u32[]{:S(2)}, u32[]{:S(2)}) collective-permute-start(bf16[2,512,128]{2,1,0:T(8,128)(2,1)S(1)} %constant_dynamic-update-slice_fusion.refs_4_), channel_id=1, source_target_pairs={{0,384},{128,0},{256,128},{384,256},{1,385},{129,1},{257,129},{385... | collective-permute-start | bytes 786440 | tf_op jit(solution)/shard_map/ppermute | solution.py:190
  24.5 28.3 %collective-permute-start = (bf16[2,512,128]{2,1,0:T(8,128)(2,1)S(1)}, bf16[2,512,128]{2,1,0:T(8,128)(2,1)S(1)}, u32[]{:S(2)}, u32[]{:S(2)}) collective-permute-start(bf16[2,512,128]{2,1,0:T(8,128)(2,1)S(1)} %constant_dynamic-update-slice_fusion.refs_4_), channel_id=1, source_target_pairs={{0,256},{128,384},{256,0},{384,128},{1,257},{129,385},{257,1},{385... | collective-permute-start | bytes 786440 | tf_op jit(solution)/shard_map/ppermute | solution.py:190
  29.6 27.9 %collective-permute-start.6 = (bf16[2,512,128]{2,1,0:T(8,128)(2,1)S(1)}, bf16[2,512,128]{2,1,0:T(8,128)(2,1)S(1)}, u32[]{:S(2)}, u32[]{:S(2)}) collective-permute-start(bf16[2,512,128]{2,1,0:T(8,128)(2,1)S(1)} %constant_dynamic-update-slice_fusion.refs_4_), channel_id=1, source_target_pairs={{0,8},{8,0},{1,9},{9,1},{2,10},{10,2},{3,11},{11,3},{4,12},{12,4},... | collective-permute-start | bytes 786440 | tf_op jit(solution)/shard_map/ppermute | solution.py:200
  34.2 29.0 %collective-permute-start.5 = (bf16[2,512,128]{2,1,0:T(8,128)(2,1)S(1)}, bf16[2,512,128]{2,1,0:T(8,128)(2,1)S(1)}, u32[]{:S(2)}, u32[]{:S(2)}) collective-permute-start(bf16[2,512,128]{2,1,0:T(8,128)(2,1)S(1)} %collective-permute-done.4.refs_4_), channel_id=1, source_target_pairs={{0,8},{8,0},{1,9},{9,1},{2,10},{10,2},{3,11},{11,3},{4,12},{12,4},... | collective-permute-start | bytes 786440 | tf_op jit(solution)/shard_map/ppermute | solution.py:202
  50.9 15.7 %collective-permute-start.3 = (bf16[2,512,128]{2,1,0:T(8,128)(2,1)S(1)}, bf16[2,512,128]{2,1,0:T(8,128)(2,1)S(1)}, u32[]{:S(2)}, u32[]{:S(2)}) collective-permute-start(bf16[2,512,128]{2,1,0:T(8,128)(2,1)S(1)} %collective-permute-done.2.refs_4_), channel_id=1, source_target_pairs={{0,8},{8,0},{1,9},{9,1},{2,10},{10,2},{3,11},{11,3},{4,12},{12,4},... | collective-permute-start | bytes 786440 | tf_op jit(solution)/shard_map/ppermute | solution.py:204
  52.9 19.1 %collective-permute-start.1 = (bf16[2,512,128]{2,1,0:T(8,128)(2,1)S(1)}, bf16[2,512,128]{2,1,0:T(8,128)(2,1)S(1)}, u32[]{:S(2)}, u32[]{:S(2)}) collective-permute-start(bf16[2,512,128]{2,1,0:T(8,128)(2,1)S(1)} %collective-permute-done.refs_4_), channel_id=1, source_target_pairs={{0,8},{8,0},{1,9},{9,1},{2,10},{10,2},{3,11},{11,3},{4,12},{12,4},... | collective-permute-start | bytes 786440 | tf_op jit(solution)/shard_map/ppermute | solution.py:206
  57.4 0.7 copy-start.2
  58.1 0.9 copy-start
  59.0 0.8 copy-start.1
  104.5 1.4 %copy-start.4 = (f32[16,8]{1,0:T(8,128)S(1)}, f32[16,8]{1,0:T(8,128)}, u32[]{:S(2)}) copy-start(f32[16,8]{1,0:T(8,128)} %get-tuple-element.19) | copy-start | bytes 1540

commit v2 on v1

v2 whole, which is shorter than its diff:
```python
import functools
import math

import jax
import jax.numpy as jnp
from jax import lax
from jax.experimental import pallas as pl
from jax.experimental.pallas import tpu as pltpu
from jax.sharding import Mesh
from jax.sharding import PartitionSpec as P


HEAD = 128
HIDE = -1e30
CTX = ("y1", "y0", "z1", "z0", "core")
TP = ("x", "yl")
ROUTE = ("z1", "z0", "x", "yl")


def prep_kernel(lens_ref, ids_ref, place_ref, hide_ref, pick_ref):
    block = pick_ref.shape[0] // 64
    y, z, core = place_ref[1], place_ref[2], place_ref[3]
    total = hide_ref.shape[1]
    row = lax.broadcasted_iota(jnp.int32, (block, 128), 0)
    lane = lax.broadcasted_iota(jnp.int32, (block, 128), 1)
    qseg = jnp.zeros((block, 128), jnp.int32)
    for a in range(8):
        first = (y * 16 + a * 2 + core) * block
        for i in range(block):
            qseg = jnp.where(lane == a * block + i, ids_ref[first + i], qseg)
    slot = lax.broadcasted_iota(jnp.int32, (total - block, 128), 0)
    for j in range(8):
        shard = ((y + 4 - j // 2) % 4) * 16 + z * 2 + (core if j % 2 == 0 else 1 - core)
        old = jnp.where(slot < lens_ref[shard], 0.0, HIDE).astype(jnp.bfloat16)
        kseg = jnp.zeros((block, 128), jnp.int32)
        for i in range(block):
            kseg = jnp.where(row == i, ids_ref[shard * block + i], kseg)
        new = jnp.where(kseg <= qseg, 0.0, HIDE).astype(jnp.bfloat16)
        hide_ref[j] = jnp.concatenate([old, new], axis=0)
    token = lax.broadcasted_iota(jnp.int32, pick_ref.shape, 0) // 8
    picked = token == lax.broadcasted_iota(jnp.int32, pick_ref.shape, 1)
    pick_ref[...] = jnp.where(picked, 1.0, 0.0).astype(jnp.bfloat16)


def prep(lens, ids, place, total):
    smem = pl.BlockSpec(memory_space=pltpu.SMEM)
    vmem = pl.BlockSpec(memory_space=pltpu.VMEM)
    return pl.pallas_call(
        prep_kernel,
        out_shape=(
            jax.ShapeDtypeStruct((8, total, 128), jnp.bfloat16),
            jax.ShapeDtypeStruct((1024, 128), jnp.bfloat16),
        ),
        in_specs=[smem, smem, smem],
        out_specs=(vmem, vmem),
        compiler_params=pltpu.CompilerParams(vmem_limit_bytes=8 << 20),
        name="prep",
    )(lens, ids, place)


def join_kernel(cache_ref, new_ref, out_ref):
    count = cache_ref.shape[1]
    for kind in range(2):
        out_ref[kind, 0:count, :] = cache_ref[kind]
        out_ref[kind, count : out_ref.shape[1], :] = new_ref[kind]


def join(cache, new):
    return pl.pallas_call(
        join_kernel,
        out_shape=jax.ShapeDtypeStruct((2, cache.shape[1] + new.shape[1], HEAD), cache.dtype),
        out_specs=pl.BlockSpec(memory_space=pltpu.VMEM),
        compiler_params=pltpu.CompilerParams(vmem_limit_bytes=4 << 20),
        name="join",
    )(cache, new)


def spread_kernel(q_ref, out_ref):
    for g in range(8):
        heads = []
        for r in range(2):
            for h in range(8):
                at = (g * 8 + h) * HEAD
                heads.append(q_ref[r : r + 1, at : at + HEAD])
        block = jnp.concatenate(heads, axis=0)
        for a in range(8):
            out_ref[a * 8 + g] = block


def spread(q):
    vmem = pl.BlockSpec(memory_space=pltpu.VMEM)
    return pl.pallas_call(
        spread_kernel,
        out_shape=jax.ShapeDtypeStruct((64, 16, HEAD), q.dtype),
        in_specs=[vmem],
        out_specs=vmem,
        compiler_params=pltpu.CompilerParams(vmem_limit_bytes=4 << 20),
        name="spread",
    )(q)


def pair_kernel(one_ref, two_ref, out_ref):
    out_ref[0] = one_ref[...]
    out_ref[1] = two_ref[...]


def pair(one, two):
    vmem = pl.BlockSpec(memory_space=pltpu.VMEM)
    return pl.pallas_call(
        pair_kernel,
        out_shape=jax.ShapeDtypeStruct((2, *one.shape), one.dtype),
        in_specs=[vmem, vmem],
        out_specs=vmem,
        compiler_params=pltpu.CompilerParams(vmem_limit_bytes=4 << 20),
        name="pair",
    )(one, two)


def attend_kernel(shards, chunks, has_state, final, *refs):
    q_ref, pick_ref, hide_ref = refs[:3]
    chunk_refs = []
    rest = list(refs[3:])
    for _ in range(chunks):
        ref = rest.pop(0)
        chunk_refs += [ref] if len(ref.shape) == 3 else [ref.at[0], ref.at[1]]
    state_ref = rest[0] if has_state else None
    out_ref, turned_ref = rest[-2:]
    rows = q_ref.shape[0]
    tile = 256
    scale = HEAD**-0.5
    factor = scale * math.log2(math.e)
    steps = [(part, which) for part in range(rows // tile) for which in range(len(shards))]

    def score(step):
        part, which = step
        cols = slice(part * tile, (part + 1) * tile)
        keys = jnp.concatenate([chunk_refs[which][0], hide_ref[shards[which]]], axis=1)
        q = jnp.concatenate([q_ref[cols, :], pick_ref[cols, :]], axis=1)
        return lax.dot_general(keys, q, (((1,), (1,)), ((), ())), preferred_element_type=jnp.float32)

    s = score(steps[0])
    for which in range(len(shards)):
        turned_ref[which] = chunk_refs[which][1].T
    acc = peak = denom = None
    for at, (part, which) in enumerate(steps):
        ahead = score(steps[at + 1]) if at + 1 < len(steps) else None
        cols = slice(part * tile, (part + 1) * tile)
        if which == 0:
            acc = peak = denom = None
            if has_state:
                acc = state_ref[0:HEAD, cols]
                peak = state_ref[HEAD : HEAD + 1, cols]
                denom = state_ref[HEAD + 1 : HEAD + 2, cols]
        m = jnp.max(s, axis=0, keepdims=True)
        e = jnp.exp2((s - m) * factor)
        l = jnp.sum(e, axis=0, keepdims=True)
        o = jnp.dot(turned_ref[which], e.astype(jnp.bfloat16), preferred_element_type=jnp.float32)
        if acc is None:
            acc, peak, denom = o, m, l
        else:
            top = jnp.maximum(peak, m)
            keep = jnp.exp2((peak - top) * factor)
            fresh = jnp.exp2((m - top) * factor)
            acc = acc * keep + o * fresh
            denom = denom * keep + l * fresh
            peak = top
        s = ahead
        if which + 1 < len(shards):
            continue
        if not final:
            out_ref[0:HEAD, cols] = acc
            out_ref[HEAD : HEAD + 1, cols] = peak
            out_ref[HEAD + 1 : HEAD + 2, cols] = denom
        else:
            acc = acc / denom
            lse = peak * scale + jnp.log(denom)
            for half in range(tile // 128):
                block = acc[:, half * 128 : (half + 1) * 128].T
                line = lse[:, half * 128 : (half + 1) * 128]
                for t in range(8):
                    to = ((part * (tile // 128) + half) * 8 + t) * 17
                    out_ref[to : to + 16, :] = block[t * 16 : (t + 1) * 16, :]
                    out_ref[to + 16 : to + 17, :] = line


def attend(shards, q, prepared, chunks, state=None, final=False):
    vmem = pl.BlockSpec(memory_space=pltpu.VMEM)
    hide, pick = prepared
    operands = [q, pick, hide, *chunks]
    aliases = {}
    shape = (1088, 128) if final else (HEAD + 8, q.shape[0])
    if state is not None:
        if not final:
            aliases = {len(operands): 0}
        operands.append(state)
    work = len(shards) * q.shape[0] * chunks[0].shape[-2]
    return pl.pallas_call(
        functools.partial(attend_kernel, tuple(shards), len(chunks), state is not None, final),
        out_shape=jax.ShapeDtypeStruct(shape, jnp.float32),
        in_specs=[vmem] * len(operands),
        out_specs=vmem,
        input_output_aliases=aliases,
        scratch_shapes=[pltpu.VMEM((len(shards), HEAD, chunks[0].shape[-2]), jnp.bfloat16)],
        cost_estimate=pl.CostEstimate(flops=4 * HEAD * work, transcendentals=work, bytes_accessed=1 << 20),
        compiler_params=pltpu.CompilerParams(vmem_limit_bytes=32 << 20),
        name="attend",
    )(*operands)


def combine_kernel(place_ref, got_ref, out_ref, lse_ref, turned_ref, line_ref):
    me = place_ref[0]
    lse = got_ref[pl.ds(16, 64, stride=17), :].reshape(8, 8, 128)
    peak = jnp.max(lse, axis=0)
    w = jnp.exp(lse - peak[None])
    denom = jnp.sum(w, axis=0)
    w = (w / denom[None]).reshape(64, 128)
    turned_ref[...] = jnp.concatenate([w, w], axis=0).T
    line_ref[...] = peak + jnp.log(denom)
    mine = turned_ref[pl.ds(pl.multiple_of(me * 16, 16), 16), :]
    for g in range(8):
        acc = None
        for z in range(8):
            at = z * 8 + g
            term = got_ref[at * 17 : at * 17 + 16, :] * mine[:, at : at + 1]
            acc = term if acc is None else acc + term
        for h in range(8):
            pair = jnp.concatenate([acc[h : h + 1], acc[8 + h : 9 + h]], axis=0)
            out_ref[:, (g * 8 + h) * 128 : (g * 8 + h + 1) * 128] = pair.astype(jnp.bfloat16)
    line = jnp.broadcast_to(line_ref[pl.ds(me, 1), :], (16, 128))
    row = lax.broadcasted_iota(jnp.int32, (16, 128), 0)
    table = line
    for i in range(1, 16):
        table = jnp.where(row == i, pltpu.roll(line, 128 - 8 * i, 1), table)
    table = jnp.concatenate([table] * 8, axis=0).T
    lse_ref[...] = table[:8, :16]


def combine(place, got):
    smem = pl.BlockSpec(memory_space=pltpu.SMEM)
    vmem = pl.BlockSpec(memory_space=pltpu.VMEM)
    return pl.pallas_call(
        combine_kernel,
        out_shape=(
            jax.ShapeDtypeStruct((2, 8192), jnp.bfloat16),
            jax.ShapeDtypeStruct((8, 16), jnp.float32),
        ),
        in_specs=[smem, vmem],
        out_specs=(vmem, vmem),
        scratch_shapes=[pltpu.VMEM((128, 128), jnp.float32), pltpu.VMEM((8, 128), jnp.float32)],
        compiler_params=pltpu.CompilerParams(vmem_limit_bytes=8 << 20),
        name="combine",
    )(place, got)


def shards_program(q_new, kv_new, kv_cache, cache_lens, segment_ids):
    y1, y0, z1, z0, core = (lax.axis_index(name) for name in CTX)
    place = jnp.stack([lax.axis_index(TP), y1 * 2 + y0, z1 * 2 + z0, core]).astype(jnp.int32)
    swap = [(0, 1), (1, 0)]

    own = join(kv_cache, kv_new)
    turn = lambda by: [(i, (i + by) % 4) for i in range(4)]
    one = lax.ppermute(own, ("y1", "y0"), turn(1))
    two = lax.ppermute(own, ("y1", "y0"), turn(2))
    three = lax.ppermute(own, ("y1", "y0"), turn(3))
    own_x = lax.ppermute(own, "core", swap)
    q = spread(q_new)
    q = lax.all_to_all(q, ROUTE, split_axis=0, concat_axis=0, tiled=True)
    q = q.reshape(1024, HEAD)
    prepared = prep(cache_lens, segment_ids, place, own.shape[1])
    two_x = lax.ppermute(two, "core", swap)
    both = pair(one, three)
    both_x = lax.ppermute(both, "core", swap)
    chunk = {0: own, 1: own_x, 2: one, 4: two, 6: three, 5: two_x, (3, 7): both_x, (2, 6): both}
    state = None
    for n, shards in enumerate(GROUPS):
        final = n + 1 == len(GROUPS)
        flat = [j for entry in shards for j in (entry if isinstance(entry, tuple) else (entry,))]
        state = attend(flat, q, prepared, [chunk[j] for j in shards], state, final=final)
    sent = state.reshape(64, 1, 2176)
    got = lax.all_to_all(sent, ROUTE, split_axis=0, concat_axis=0, tiled=True)
    out, lse = combine(place, got.reshape(1088, HEAD))
    return out, lse.T


GROUPS = [[0, 1], [4, 5], [(2, 6)], [(3, 7)]]


def solution(mesh):
    fine = Mesh(mesh.devices.reshape(2, 2, 4, 2, 2, 4, 2), CTX + TP)
    rows = P(CTX + TP, None)
    kv = P(None, CTX, TP)
    return jax.shard_map(
        shards_program,
        mesh=fine,
        in_specs=(rows, kv, kv, P(), P()),
        out_specs=(rows, P(CTX, TP)),
        check_vma=False,
    )
```

time: 107 us -> 89.3 us (0.83)
  the two profiles are of different devices: /device:TPU:16 before, /device:TPU:9 now
where the time goes in v2:
time: 89.3 us; the launch traced here: 88.8 us
  starting transfers between devices  37 us (41%)
  blocking collectives  28.8 us (32%)
  Pallas kernels  12.6 us (14%)
  waiting for transfers between devices  7.21 us (8%)
  local copies, waits for them, and re-layouts  2.24 us (3%)
    all_to_all x1, blocking collectives, shards_program(): got = lax.all_to_all(sent, ROUTE, split_axis=0, concat_axis=0, tiled=True)  28.8 us
    all_to_all x1, starting transfers between devices, shards_program(): q = lax.all_to_all(q, ROUTE, split_axis=0, concat_axis=0, tiled=True)  14.2 us
    pallas_call x4, Pallas kernels, attend(): pl.pallas_call(functools.partial(attend_kernel, tuple(shards), len(chunks...  9.08 us
    ppermute x1, waiting for transfers between devices, shards_program(): two = lax.ppermute(own, ('y1', 'y0'), turn(2))  7.2 us
    ppermute x1, starting transfers between devices, shards_program(): two = lax.ppermute(own, ('y1', 'y0'), turn(2))  6.55 us
    ppermute x1, starting transfers between devices, shards_program(): one = lax.ppermute(own, ('y1', 'y0'), turn(1))  4.22 us
    ppermute x1, starting transfers between devices, shards_program(): both_x = lax.ppermute(both, 'core', swap)  3.98 us
    ppermute x1, starting transfers between devices, shards_program(): three = lax.ppermute(own, ('y1', 'y0'), turn(3))  3.17 us
  transfers between devices with their start and end apart: 7, of which 1 were waited for; matrix products, arithmetic and copies ran while one was open for 0% of the time, Pallas kernels for 10%

profile of v2, /device:TPU:9, one launch (start us, length us, event | category | flops | bytes accessed | tf_op | source)
XLA Modules:
  0.0 88.8 jit_solution(14538238466592846495)
XLA Ops:
  0.6 0.0 copy-start
  0.6 0.9 %copy-done = bf16[2,496,128]{2,1,0:T(8,128)(2,1)S(1)} copy-done((bf16[2,496,128]{2,1,0:T(8,128)(2,1)S(1)}, bf16[2,496,128]{2,1,0:T(8,128)(2,1)}, u32[]{:S(2)}) %copy-start) | copy-done | bytes 253976
  1.6 0.0 copy-start.2
  1.6 0.7 copy-done.2
  2.3 4.2 %collective-permute-start = (bf16[2,512,128]{2,1,0:T(8,128)(2,1)S(1)}, bf16[2,512,128]{2,1,0:T(8,128)(2,1)S(1)}, u32[]{:S(2)}, u32[]{:S(2)}) collective-permute-start(bf16[2,512,128]{2,1,0:T(8,128)(2,1)S(1)} %join.1.refs_3_), channel_id=1, source_target_pairs={{0,128},{128,256},{256,384},{384,0},{1,129},{129,257},{257,385},{3... | collective-permute-start | bytes 786440 | tf_op jit(solution)/shard_map/ppermute | solution.py:262
  6.5 3.2 %collective-permute-start.1 = (bf16[2,512,128]{2,1,0:T(8,128)(2,1)S(1)}, bf16[2,512,128]{2,1,0:T(8,128)(2,1)S(1)}, u32[]{:S(2)}, u32[]{:S(2)}) collective-permute-start(bf16[2,512,128]{2,1,0:T(8,128)(2,1)S(1)} %join.1.refs_3_), channel_id=1, source_target_pairs={{0,384},{128,0},{256,128},{384,256},{1,385},{129,1},{257,129},{385... | collective-permute-start | bytes 786440 | tf_op jit(solution)/shard_map/ppermute | solution.py:264
  9.7 0.0 copy-done.1
  9.7 0.8 spread.1
  10.5 14.2 %all-to-all-start = ((bf16[64,16,128]{2,1,0:T(8,128)(2,1)}), bf16[64,16,128]{2,1,0:T(8,128)(2,1)S(1)}, u32[]{:S(2)}, u32[]{:S(2)}) async-start(bf16[64,16,128]{2,1,0:T(8,128)(2,1)} %spread.1), calls=%async_computation | async-start | bytes 524288 | tf_op jit(solution)/shard_map/all_to_all | solution.py:267
  24.7 6.6 %collective-permute-start.3 = (bf16[2,512,128]{2,1,0:T(8,128)(2,1)S(1)}, bf16[2,512,128]{2,1,0:T(8,128)(2,1)S(1)}, u32[]{:S(2)}, u32[]{:S(2)}) collective-permute-start(bf16[2,512,128]{2,1,0:T(8,128)(2,1)S(1)} %join.1.refs_3_), channel_id=1, source_target_pairs={{0,256},{128,384},{256,0},{384,128},{1,257},{129,385},{257,1},{385... | collective-permute-start | bytes 786440 | tf_op jit(solution)/shard_map/ppermute | solution.py:263
  31.3 0.0 collective-permute-done.one_ref
  31.3 0.0 collective-permute-done.1.two_ref
  31.4 4.0 %collective-permute-start.2 = (bf16[2,2,512,128]{3,2,1,0:T(8,128)(2,1)S(1)}, bf16[2,2,512,128]{3,2,1,0:T(8,128)(2,1)S(1)}, u32[]{:S(2)}, u32[]{:S(2)}) collective-permute-start(bf16[2,2,512,128]{3,2,1,0:T(8,128)(2,1)S(1)} %pair.1.refs_3_), channel_id=1, source_target_pairs={{0,8},{8,0},{1,9},{9,1},{2,10},{10,2},{3,11},{11,3},{4,12},{12,4},... | collective-permute-start | bytes 1572872 | tf_op jit(solution)/shard_map/ppermute | solution.py:272
  35.4 1.9 %collective-permute-start.5 = (bf16[2,512,128]{2,1,0:T(8,128)(2,1)S(1)}, bf16[2,512,128]{2,1,0:T(8,128)(2,1)}, u32[]{:S(2)}, u32[]{:S(2)}) collective-permute-start(bf16[2,512,128]{2,1,0:T(8,128)(2,1)S(1)} %join.1.refs_3_), channel_id=1, source_target_pairs={{0,8},{8,0},{1,9},{9,1},{2,10},{10,2},{3,11},{11,3},{4,12},{12,4},... | collective-permute-start | bytes 786440 | tf_op jit(solution)/shard_map/ppermute | solution.py:265
  37.3 7.2 %collective-permute-done.3.refs_3_ = bf16[2,512,128]{2,1,0:T(8,128)(2,1)S(1)} collective-permute-done((bf16[2,512,128]{2,1,0:T(8,128)(2,1)S(1)}, bf16[2,512,128]{2,1,0:T(8,128)(2,1)S(1)}, u32[]{:S(2)}, u32[]{:S(2)}) %collective-permute-start.3) | collective-permute-done | bytes 262176 | tf_op jit(solution)/shard_map/ppermute | solution.py:263
  44.5 2.9 %collective-permute-start.4 = (bf16[2,512,128]{2,1,0:T(8,128)(2,1)S(1)}, bf16[2,512,128]{2,1,0:T(8,128)(2,1)S(1)}, u32[]{:S(2)}, u32[]{:S(2)}) collective-permute-start(bf16[2,512,128]{2,1,0:T(8,128)(2,1)S(1)} %collective-permute-done.3.refs_3_), channel_id=1, source_target_pairs={{0,8},{8,0},{1,9},{9,1},{2,10},{10,2},{3,11},{11,3},{4,12},{12,4},... | collective-permute-start | bytes 786440 | tf_op jit(solution)/shard_map/ppermute | solution.py:270
  47.4 0.0 copy-start.3
  47.4 0.0 copy-start.4
  47.4 0.1 pad_add_fusion.place_ref
  47.5 0.6 copy-done.3
  48.1 0.0 copy-done.4
  48.1 1.1 %prep.1 = (bf16[8,512,128]{2,1,0:T(8,128)(2,1)S(1)}, bf16[1024,128]{1,0:T(8,128)(2,1)S(1)}) custom-call(s32[64]{0:T(128)S(1)} %copy-done.4, s32[1024]{0:T(1024)S(1)} %copy-done.3, s32[4]{0:T(128)S(1)} %pad_add_fusion.place_ref), custom_call_target="tpu_custom_call" | custom-call | tf_op jit(solution)/shard_map/prep/pallas_call | solution.py:48
  49.2 0.0 collective-permute-done.5.refs_4_
  49.2 0.0 all-to-all-done
  49.2 3.0 %attend.4.refs_5_ = f32[136,1024]{1,0:T(8,128)S(1)} custom-call(bf16[1024,128]{1,0:T(8,128)(2,1)S(1)} %bitcast.8, bf16[1024,128]{1,0:T(8,128)(2,1)S(1)} %get-tuple-element.6.refs_1_, bf16[8,512,128]{2,1,0:T(8,128)(2,1)S(1)} %get-tuple-element.7.refs_2_, bf16[2,512,128]{2,1,0:T(8,128)(2,1)S(1)} %join.1.refs_3_, ...), custom_call_target="tpu_custom_call" | custom-call | flops 536870912 | bytes 1048576 | tf_op jit(solution)/shard_map/attend/pallas_call | solution.py:197
  52.1 0.0 collective-permute-done.4.refs_4_
  52.2 2.0 %attend.5.refs_4_ = f32[136,1024]{1,0:T(8,128)S(1)} custom-call(bf16[1024,128]{1,0:T(8,128)(2,1)S(1)} %bitcast.9, bf16[1024,128]{1,0:T(8,128)(2,1)S(1)} %get-tuple-element.6.refs_1_, bf16[8,512,128]{2,1,0:T(8,128)(2,1)S(1)} %get-tuple-element.7.refs_2_, bf16[2,512,128]{2,1,0:T(8,128)(2,1)S(1)} %collective-permute-done.3.refs_3_, ...), custom_call_target="tpu_custom_call", output_to_operand_aliasing={{}: (5, {})} | custom-call | flops 536870912 | bytes 1048576 | tf_op jit(solution)/shard_map/attend/pallas_call | solution.py:197
  54.2 2.0 %attend.6.refs_4_ = f32[136,1024]{1,0:T(8,128)S(1)} custom-call(bf16[1024,128]{1,0:T(8,128)(2,1)S(1)} %bitcast.10, bf16[1024,128]{1,0:T(8,128)(2,1)S(1)} %get-tuple-element.6.refs_1_, bf16[8,512,128]{2,1,0:T(8,128)(2,1)S(1)} %get-tuple-element.7.refs_2_, bf16[2,2,512,128]{3,2,1,0:T(8,128)(2,1)S(1)} %pair.1.refs_3_, ...), custom_call_target="tpu_custom_call", output_to_operand_aliasing={{}: (4, {})} | custom-call | flops 536870912 | bytes 1048576 | tf_op jit(solution)/shard_map/attend/pallas_call | solution.py:197
  56.2 0.0 collective-permute-done.2.refs_3_
  56.2 2.1 %attend.7 = f32[1088,128]{1,0:T(8,128)S(1)} custom-call(bf16[1024,128]{1,0:T(8,128)(2,1)S(1)} %bitcast.11, bf16[1024,128]{1,0:T(8,128)(2,1)S(1)} %get-tuple-element.6.refs_1_, bf16[8,512,128]{2,1,0:T(8,128)(2,1)S(1)} %get-tuple-element.7.refs_2_, bf16[2,2,512,128]{3,2,1,0:T(8,128)(2,1)S(1)} %collective-permute-done.2.refs_3_, f32[136,1024]{1,0:T(8,128)S(1)} %attend.6.refs_4_), custom_call_target="tpu_custom_call" | custom-call | flops 536870912 | bytes 1048576 | tf_op jit(solution)/shard_map/attend/pallas_call | solution.py:197
  58.3 28.8 %all_to_all.10 = f32[64,1,2176]{2,1,0:T(1,128)S(1)} all-to-all(f32[64,1,2176]{2,1,0:T(1,128)S(1)} %bitcast.12), channel_id=1, replica_groups=mesh['y1'=2,'y0'=2,'z1'=4,'z0'=2,'core'=2,'x'=4,'yl'=2] {'z1','z0','x','..., dimensions={0} | all-to-all | bytes 1114112 | tf_op jit(solution)/shard_map/all_to_all | solution.py:280
  87.1 1.6 %combine.1 = (bf16[2,8192]{1,0:T(2,128)(2,1)}, f32[8,16]{1,0:T(8,128)}) custom-call(s32[4]{0:T(128)S(1)} %pad_add_fusion.place_ref, f32[1088,128]{1,0:T(8,128)S(1)} %bitcast.13), custom_call_target="tpu_custom_call" | custom-call | tf_op jit(solution)/shard_map/combine/pallas_call | solution.py:241
  (3 shorter events, 0.1 us)
Async XLA Ops:
  0.6 0.9 %copy-start = (bf16[2,496,128]{2,1,0:T(8,128)(2,1)S(1)}, bf16[2,496,128]{2,1,0:T(8,128)(2,1)}, u32[]{:S(2)}) copy-start(bf16[2,496,128]{2,1,0:T(8,128)(2,1)} %cache_ref.1) | copy-start | bytes 761860
  1.6 0.7 copy-start.2
  2.3 7.4 %copy-start.1 = (bf16[2,8192]{1,0:T(2,128)(2,1)S(1)}, bf16[2,8192]{1,0:T(2,128)(2,1)}, u32[]{:S(2)}) copy-start(bf16[2,8192]{1,0:T(2,128)(2,1)} %q_ref.1) | copy-start | bytes 98308
  2.3 29.0 %collective-permute-start = (bf16[2,512,128]{2,1,0:T(8,128)(2,1)S(1)}, bf16[2,512,128]{2,1,0:T(8,128)(2,1)S(1)}, u32[]{:S(2)}, u32[]{:S(2)}) collective-permute-start(bf16[2,512,128]{2,1,0:T(8,128)(2,1)S(1)} %join.1.refs_3_), channel_id=1, source_target_pairs={{0,128},{128,256},{256,384},{384,0},{1,129},{129,257},{257,385},{3... | collective-permute-start | bytes 786440 | tf_op jit(solution)/shard_map/ppermute | solution.py:262
  6.5 24.8 %collective-permute-start.1 = (bf16[2,512,128]{2,1,0:T(8,128)(2,1)S(1)}, bf16[2,512,128]{2,1,0:T(8,128)(2,1)S(1)}, u32[]{:S(2)}, u32[]{:S(2)}) collective-permute-start(bf16[2,512,128]{2,1,0:T(8,128)(2,1)S(1)} %join.1.refs_3_), channel_id=1, source_target_pairs={{0,384},{128,0},{256,128},{384,256},{1,385},{129,1},{257,129},{385... | collective-permute-start | bytes 786440 | tf_op jit(solution)/shard_map/ppermute | solution.py:264
  10.5 38.7 %all-to-all-start = ((bf16[64,16,128]{2,1,0:T(8,128)(2,1)}), bf16[64,16,128]{2,1,0:T(8,128)(2,1)S(1)}, u32[]{:S(2)}, u32[]{:S(2)}) async-start(bf16[64,16,128]{2,1,0:T(8,128)(2,1)} %spread.1), calls=%async_computation | async-start | bytes 524288 | tf_op jit(solution)/shard_map/all_to_all | solution.py:267
  24.7 19.7 %collective-permute-start.3 = (bf16[2,512,128]{2,1,0:T(8,128)(2,1)S(1)}, bf16[2,512,128]{2,1,0:T(8,128)(2,1)S(1)}, u32[]{:S(2)}, u32[]{:S(2)}) collective-permute-start(bf16[2,512,128]{2,1,0:T(8,128)(2,1)S(1)} %join.1.refs_3_), channel_id=1, source_target_pairs={{0,256},{128,384},{256,0},{384,128},{1,257},{129,385},{257,1},{385... | collective-permute-start | bytes 786440 | tf_op jit(solution)/shard_map/ppermute | solution.py:263
  31.4 24.8 %collective-permute-start.2 = (bf16[2,2,512,128]{3,2,1,0:T(8,128)(2,1)S(1)}, bf16[2,2,512,128]{3,2,1,0:T(8,128)(2,1)S(1)}, u32[]{:S(2)}, u32[]{:S(2)}) collective-permute-start(bf16[2,2,512,128]{3,2,1,0:T(8,128)(2,1)S(1)} %pair.1.refs_3_), channel_id=1, source_target_pairs={{0,8},{8,0},{1,9},{9,1},{2,10},{10,2},{3,11},{11,3},{4,12},{12,4},... | collective-permute-start | bytes 1572872 | tf_op jit(solution)/shard_map/ppermute | solution.py:272
  35.4 13.8 %collective-permute-start.5 = (bf16[2,512,128]{2,1,0:T(8,128)(2,1)S(1)}, bf16[2,512,128]{2,1,0:T(8,128)(2,1)}, u32[]{:S(2)}, u32[]{:S(2)}) collective-permute-start(bf16[2,512,128]{2,1,0:T(8,128)(2,1)S(1)} %join.1.refs_3_), channel_id=1, source_target_pairs={{0,8},{8,0},{1,9},{9,1},{2,10},{10,2},{3,11},{11,3},{4,12},{12,4},... | collective-permute-start | bytes 786440 | tf_op jit(solution)/shard_map/ppermute | solution.py:265
  44.5 7.7 %collective-permute-start.4 = (bf16[2,512,128]{2,1,0:T(8,128)(2,1)S(1)}, bf16[2,512,128]{2,1,0:T(8,128)(2,1)S(1)}, u32[]{:S(2)}, u32[]{:S(2)}) collective-permute-start(bf16[2,512,128]{2,1,0:T(8,128)(2,1)S(1)} %collective-permute-done.3.refs_3_), channel_id=1, source_target_pairs={{0,8},{8,0},{1,9},{9,1},{2,10},{10,2},{3,11},{11,3},{4,12},{12,4},... | collective-permute-start | bytes 786440 | tf_op jit(solution)/shard_map/ppermute | solution.py:270
  47.4 0.7 copy-start.3
  47.4 0.7 copy-start.4

commit v3 on v2

--- a/solution.py
+++ b/solution.py
@@ -12,48 +12,52 @@
 
 HEAD = 128
 HIDE = -1e30
+SENT = 10
 CTX = ("y1", "y0", "z1", "z0", "core")
 TP = ("x", "yl")
 ROUTE = ("z1", "z0", "x", "yl")
 
 
-def prep_kernel(lens_ref, ids_ref, place_ref, hide_ref, pick_ref):
+def prep_kernel(lens_ref, ids_ref, place_ref, filled_ref, kseg_ref, qseg_ref, pick_ref):
     block = pick_ref.shape[0] // 64
     y, z, core = place_ref[1], place_ref[2], place_ref[3]
-    total = hide_ref.shape[1]
     row = lax.broadcasted_iota(jnp.int32, (block, 128), 0)
-    lane = lax.broadcasted_iota(jnp.int32, (block, 128), 1)
-    qseg = jnp.zeros((block, 128), jnp.int32)
+    lane = lax.broadcasted_iota(jnp.int32, (8, 128), 1)
+    which = lax.broadcasted_iota(jnp.int32, (8, 128), 0)
+    qseg = jnp.zeros((8, 128), jnp.int32)
     for a in range(8):
         first = (y * 16 + a * 2 + core) * block
         for i in range(block):
             qseg = jnp.where(lane == a * block + i, ids_ref[first + i], qseg)
-    slot = lax.broadcasted_iota(jnp.int32, (total - block, 128), 0)
+    qseg_ref[...] = qseg
+    filled = jnp.zeros((8, 128), jnp.int32)
     for j in range(8):
         shard = ((y + 4 - j // 2) % 4) * 16 + z * 2 + (core if j % 2 == 0 else 1 - core)
-        old = jnp.where(slot < lens_ref[shard], 0.0, HIDE).astype(jnp.bfloat16)
+        filled = jnp.where(which == j, lens_ref[shard], filled)
         kseg = jnp.zeros((block, 128), jnp.int32)
         for i in range(block):
             kseg = jnp.where(row == i, ids_ref[shard * block + i], kseg)
-        new = jnp.where(kseg <= qseg, 0.0, HIDE).astype(jnp.bfloat16)
-        hide_ref[j] = jnp.concatenate([old, new], axis=0)
+        kseg_ref[j] = kseg
+    filled_ref[...] = filled
     token = lax.broadcasted_iota(jnp.int32, pick_ref.shape, 0) // 8
     picked = token == lax.broadcasted_iota(jnp.int32, pick_ref.shape, 1)
     pick_ref[...] = jnp.where(picked, 1.0, 0.0).astype(jnp.bfloat16)
 
 
-def prep(lens, ids, place, total):
+def prep(lens, ids, place):
     smem = pl.BlockSpec(memory_space=pltpu.SMEM)
     vmem = pl.BlockSpec(memory_space=pltpu.VMEM)
     return pl.pallas_call(
         prep_kernel,
         out_shape=(
-            jax.ShapeDtypeStruct((8, total, 128), jnp.bfloat16),
+            jax.ShapeDtypeStruct((8, 128), jnp.int32),
+            jax.ShapeDtypeStruct((8, 16, 128), jnp.int32),
+            jax.ShapeDtypeStruct((8, 128), jnp.int32),
             jax.ShapeDtypeStruct((1024, 128), jnp.bfloat16),
         ),
         in_specs=[smem, smem, smem],
-        out_specs=(vmem, vmem),
-        compiler_params=pltpu.CompilerParams(vmem_limit_bytes=8 << 20),
+        out_specs=(vmem, vmem, vmem, vmem),
+        compiler_params=pltpu.CompilerParams(vmem_limit_bytes=4 << 20),
         name="prep",
     )(lens, ids, place)
 
@@ -99,42 +103,49 @@
     )(q)
 
 
-def pair_kernel(one_ref, two_ref, out_ref):
-    out_ref[0] = one_ref[...]
-    out_ref[1] = two_ref[...]
-
-
-def pair(one, two):
+def pair_kernel(*refs):
+    for n, ref in enumerate(refs[:-1]):
+        refs[-1][n] = ref[...]
+
+
+def pair(*chunks):
     vmem = pl.BlockSpec(memory_space=pltpu.VMEM)
     return pl.pallas_call(
         pair_kernel,
-        out_shape=jax.ShapeDtypeStruct((2, *one.shape), one.dtype),
-        in_specs=[vmem, vmem],
+        out_shape=jax.ShapeDtypeStruct((len(chunks), *chunks[0].shape), chunks[0].dtype),
+        in_specs=[vmem] * len(chunks),
         out_specs=vmem,
         compiler_params=pltpu.CompilerParams(vmem_limit_bytes=4 << 20),
         name="pair",
-    )(one, two)
+    )(*chunks)
 
 
 def attend_kernel(shards, chunks, has_state, final, *refs):
-    q_ref, pick_ref, hide_ref = refs[:3]
+    q_ref, filled_ref, kseg_ref, qseg_ref, pick_ref = refs[:5]
     chunk_refs = []
-    rest = list(refs[3:])
+    rest = list(refs[5:])
     for _ in range(chunks):
         ref = rest.pop(0)
-        chunk_refs += [ref] if len(ref.shape) == 3 else [ref.at[0], ref.at[1]]
+        chunk_refs += [ref] if len(ref.shape) == 3 else [ref.at[n] for n in range(ref.shape[0])]
     state_ref = rest[0] if has_state else None
-    out_ref, turned_ref = rest[-2:]
+    out_ref, turned_ref, hide_ref = rest[-3:]
     rows = q_ref.shape[0]
     tile = 256
     scale = HEAD**-0.5
     factor = scale * math.log2(math.e)
     steps = [(part, which) for part in range(rows // tile) for which in range(len(shards))]
 
+    block = kseg_ref.shape[1]
+    slot = lax.broadcasted_iota(jnp.int32, (hide_ref.shape[1] - block, HEAD), 0)
+    for which, j in enumerate(shards):
+        old = jnp.where(slot < filled_ref[j : j + 1, :], 0.0, HIDE).astype(jnp.bfloat16)
+        new = jnp.where(kseg_ref[j] <= qseg_ref[0:1, :], 0.0, HIDE).astype(jnp.bfloat16)
+        hide_ref[which] = jnp.concatenate([old, new], axis=0)
+
     def score(step):
         part, which = step
         cols = slice(part * tile, (part + 1) * tile)
-        keys = jnp.concatenate([chunk_refs[which][0], hide_ref[shards[which]]], axis=1)
+        keys = jnp.concatenate([chunk_refs[which][0], hide_ref[which]], axis=1)
         q = jnp.concatenate([q_ref[cols, :], pick_ref[cols, :]], axis=1)
         return lax.dot_general(keys, q, (((1,), (1,)), ((), ())), preferred_element_type=jnp.float32)
 
@@ -172,23 +183,30 @@
             out_ref[HEAD : HEAD + 1, cols] = peak
             out_ref[HEAD + 1 : HEAD + 2, cols] = denom
         else:
-            acc = acc / denom
-            lse = peak * scale + jnp.log(denom)
+            size = jnp.max(jnp.abs(acc), axis=0, keepdims=True) / denom
+            power = jnp.ceil(jnp.log2(jnp.maximum(size, 1e-33)) + 0.001)
+            acc = jnp.floor(acc * (jnp.exp2(15.0 - power) / denom) + 0.5)
+            lse = jnp.floor((peak * scale + jnp.log(denom)) * 65536.0 + 0.5).astype(jnp.int32)
+            power = power.astype(jnp.int32)
             for half in range(tile // 128):
-                block = acc[:, half * 128 : (half + 1) * 128].T
-                line = lse[:, half * 128 : (half + 1) * 128]
+                lanes = slice(half * 128, (half + 1) * 128)
+                block = acc[:, lanes].T.astype(jnp.int32)
                 for t in range(8):
-                    to = ((part * (tile // 128) + half) * 8 + t) * 17
-                    out_ref[to : to + 16, :] = block[t * 16 : (t + 1) * 16, :]
-                    out_ref[to + 16 : to + 17, :] = line
+                    to = ((part * (tile // 128) + half) * 8 + t) * SENT
+                    upper = block[t * 16 : t * 16 + 8, :]
+                    lower = block[t * 16 + 8 : t * 16 + 16, :]
+                    out_ref[to : to + 8, :] = (upper << 16) | (lower & 0xFFFF)
+                    out_ref[to + 8 : to + 9, :] = lse[:, lanes]
+                    out_ref[to + 9 : to + 10, :] = power[:, lanes]
 
 
 def attend(shards, q, prepared, chunks, state=None, final=False):
     vmem = pl.BlockSpec(memory_space=pltpu.VMEM)
-    hide, pick = prepared
-    operands = [q, pick, hide, *chunks]
+    operands = [q, *prepared, *chunks]
     aliases = {}
-    shape = (1088, 128) if final else (HEAD + 8, q.shape[0])
+    shape = jax.ShapeDtypeStruct((HEAD + 8, q.shape[0]), jnp.float32)
+    if final:
+        shape = jax.ShapeDtypeStruct((64 * SENT, 128), jnp.int32)
     if state is not None:
         if not final:
             aliases = {len(operands): 0}
@@ -196,36 +214,44 @@
     work = len(shards) * q.shape[0] * chunks[0].shape[-2]
     return pl.pallas_call(
         functools.partial(attend_kernel, tuple(shards), len(chunks), state is not None, final),
-        out_shape=jax.ShapeDtypeStruct(shape, jnp.float32),
+        out_shape=shape,
         in_specs=[vmem] * len(operands),
         out_specs=vmem,
         input_output_aliases=aliases,
-        scratch_shapes=[pltpu.VMEM((len(shards), HEAD, chunks[0].shape[-2]), jnp.bfloat16)],
+        scratch_shapes=[
+            pltpu.VMEM((len(shards), HEAD, chunks[0].shape[-2]), jnp.bfloat16),
+            pltpu.VMEM((len(shards), chunks[0].shape[-2], HEAD), jnp.bfloat16),
+        ],
         cost_estimate=pl.CostEstimate(flops=4 * HEAD * work, transcendentals=work, bytes_accessed=1 << 20),
-        compiler_params=pltpu.CompilerParams(vmem_limit_bytes=32 << 20),
+        compiler_params=pltpu.CompilerParams(vmem_limit_bytes=16 << 20),
         name="attend",
     )(*operands)
 
 
 def combine_kernel(place_ref, got_ref, out_ref, lse_ref, turned_ref, line_ref):
     me = place_ref[0]
-    lse = got_ref[pl.ds(16, 64, stride=17), :].reshape(8, 8, 128)
+    lse = got_ref[pl.ds(8, 64, stride=SENT), :].astype(jnp.float32) * (1.0 / 65536.0)
+    power = got_ref[pl.ds(9, 64, stride=SENT), :].astype(jnp.float32) - 15.0
+    lse = lse.reshape(8, 8, 128)
     peak = jnp.max(lse, axis=0)
     w = jnp.exp(lse - peak[None])
     denom = jnp.sum(w, axis=0)
-    w = (w / denom[None]).reshape(64, 128)
+    w = (w / denom[None]).reshape(64, 128) * jnp.exp2(power)
     turned_ref[...] = jnp.concatenate([w, w], axis=0).T
     line_ref[...] = peak + jnp.log(denom)
     mine = turned_ref[pl.ds(pl.multiple_of(me * 16, 16), 16), :]
     for g in range(8):
-        acc = None
-        for z in range(8):
-            at = z * 8 + g
-            term = got_ref[at * 17 : at * 17 + 16, :] * mine[:, at : at + 1]
-            acc = term if acc is None else acc + term
+        tops = bottoms = None
+        for a in range(8):
+            at = a * 8 + g
+            word = got_ref[at * SENT : at * SENT + 8, :]
+            top = (word >> 16).astype(jnp.float32) * mine[:8, at : at + 1]
+            bottom = ((word << 16) >> 16).astype(jnp.float32) * mine[8:, at : at + 1]
+            tops = top if tops is None else tops + top
+            bottoms = bottom if bottoms is None else bottoms + bottom
         for h in range(8):
-            pair = jnp.concatenate([acc[h : h + 1], acc[8 + h : 9 + h]], axis=0)
-            out_ref[:, (g * 8 + h) * 128 : (g * 8 + h + 1) * 128] = pair.astype(jnp.bfloat16)
+            rows = jnp.concatenate([tops[h : h + 1], bottoms[h : h + 1]], axis=0)
+            out_ref[:, (g * 8 + h) * HEAD : (g * 8 + h + 1) * HEAD] = rows.astype(jnp.bfloat16)
     line = jnp.broadcast_to(line_ref[pl.ds(me, 1), :], (16, 128))
     row = lax.broadcasted_iota(jnp.int32, (16, 128), 0)
     table = line
@@ -260,29 +286,28 @@
     own = join(kv_cache, kv_new)
     turn = lambda by: [(i, (i + by) % 4) for i in range(4)]
     one = lax.ppermute(own, ("y1", "y0"), turn(1))
-    two = lax.ppermute(own, ("y1", "y0"), turn(2))
     three = lax.ppermute(own, ("y1", "y0"), turn(3))
-    own_x = lax.ppermute(own, "core", swap)
+    two = lax.ppermute(one, ("y1", "y0"), turn(1))
     q = spread(q_new)
     q = lax.all_to_all(q, ROUTE, split_axis=0, concat_axis=0, tiled=True)
     q = q.reshape(1024, HEAD)
-    prepared = prep(cache_lens, segment_ids, place, own.shape[1])
-    two_x = lax.ppermute(two, "core", swap)
-    both = pair(one, three)
-    both_x = lax.ppermute(both, "core", swap)
-    chunk = {0: own, 1: own_x, 2: one, 4: two, 6: three, 5: two_x, (3, 7): both_x, (2, 6): both}
+    prepared = prep(cache_lens, segment_ids, place)
+    both0 = pair(own, one, three)
+    sent0 = lax.ppermute(both0, "core", swap)
+    sent1 = lax.ppermute(two, "core", swap)
+    chunk = {0: own, 2: one, 4: two, 6: three, (1, 3, 7): sent0, (0, 2, 6): both0, 5: sent1}
     state = None
     for n, shards in enumerate(GROUPS):
         final = n + 1 == len(GROUPS)
         flat = [j for entry in shards for j in (entry if isinstance(entry, tuple) else (entry,))]
         state = attend(flat, q, prepared, [chunk[j] for j in shards], state, final=final)
-    sent = state.reshape(64, 1, 2176)
+    sent = state.reshape(64, 1, SENT * 128)
     got = lax.all_to_all(sent, ROUTE, split_axis=0, concat_axis=0, tiled=True)
-    out, lse = combine(place, got.reshape(1088, HEAD))
+    out, lse = combine(place, got.reshape(64 * SENT, 128))
     return out, lse.T
 
 
-GROUPS = [[0, 1], [4, 5], [(2, 6)], [(3, 7)]]
+GROUPS = [[(0, 2, 6)], [(1, 3, 7)], [4], [5]]
 
 
 def solution(mesh):

time: 89.3 us -> 98.5 us (1.10)
  the two profiles are of different devices: /device:TPU:9 before, /device:TPU:16 now
where the time goes in v3:
time: 98.5 us; the launch traced here: 98 us
  starting transfers between devices  29.8 us (30%)
  waiting for transfers between devices  27.5 us (28%)
  blocking collectives  25.8 us (26%)
  Pallas kernels  11.8 us (12%)
  local copies, waits for them, and re-layouts  2.24 us (2%)
    all_to_all x1, blocking collectives, shards_program(): got = lax.all_to_all(sent, ROUTE, split_axis=0, concat_axis=0, tiled=True)  25.8 us
    ppermute x1, waiting for transfers between devices, shards_program(): two = lax.ppermute(one, ('y1', 'y0'), turn(1))  14.7 us
    all_to_all x1, starting transfers between devices, shards_program(): q = lax.all_to_all(q, ROUTE, split_axis=0, concat_axis=0, tiled=True)  14.6 us
    pallas_call x4, Pallas kernels, attend(): pl.pallas_call(functools.partial(attend_kernel, tuple(shards), len(chunks...  8.51 us
    ppermute x1, waiting for transfers between devices, shards_program(): one = lax.ppermute(own, ('y1', 'y0'), turn(1))  7.16 us
    ppermute x1, starting transfers between devices, shards_program(): one = lax.ppermute(own, ('y1', 'y0'), turn(1))  5.71 us
    ppermute x1, waiting for transfers between devices, shards_program(): three = lax.ppermute(own, ('y1', 'y0'), turn(3))  5.65 us
    ppermute x1, starting transfers between devices, shards_program(): three = lax.ppermute(own, ('y1', 'y0'), turn(3))  3.8 us
  transfers between devices with their start and end apart: 6, of which 3 were waited for; matrix products, arithmetic and copies ran while one was open for 0% of the time, Pallas kernels for 9%

profile of v3, /device:TPU:16, one launch (start us, length us, event | category | flops | bytes accessed | tf_op | source)
XLA Modules:
  0.0 98.0 jit_solution(6130869173711771442)
XLA Ops:
  0.6 0.0 copy-start
  0.6 0.9 copy-done
  1.6 0.0 copy-start.2
  1.6 0.7 copy-done.2
  2.3 0.0 copy-start.1
  2.3 5.7 %collective-permute-start = (bf16[2,512,128]{2,1,0:T(8,128)(2,1)S(1)}, bf16[2,512,128]{2,1,0:T(8,128)(2,1)S(1)}, u32[]{:S(2)}, u32[]{:S(2)}) collective-permute-start(bf16[2,512,128]{2,1,0:T(8,128)(2,1)S(1)} %join.1.refs_0_), channel_id=1, source_target_pairs={{0,128},{128,256},{256,384},{384,0},{1,129},{129,257},{257,385},{3... | collective-permute-start | bytes 786440 | tf_op jit(solution)/shard_map/ppermute | solution.py:288
  8.0 3.8 %collective-permute-start.3 = (bf16[2,512,128]{2,1,0:T(8,128)(2,1)S(1)}, bf16[2,512,128]{2,1,0:T(8,128)(2,1)S(1)}, u32[]{:S(2)}, u32[]{:S(2)}) collective-permute-start(bf16[2,512,128]{2,1,0:T(8,128)(2,1)S(1)} %join.1.refs_0_), channel_id=1, source_target_pairs={{0,384},{128,0},{256,128},{384,256},{1,385},{129,1},{257,129},{385... | collective-permute-start | bytes 786440 | tf_op jit(solution)/shard_map/ppermute | solution.py:289
  11.8 7.2 %collective-permute-done.refs_1_ = bf16[2,512,128]{2,1,0:T(8,128)(2,1)S(1)} collective-permute-done((bf16[2,512,128]{2,1,0:T(8,128)(2,1)S(1)}, bf16[2,512,128]{2,1,0:T(8,128)(2,1)S(1)}, u32[]{:S(2)}, u32[]{:S(2)}) %collective-permute-start) | collective-permute-done | bytes 262176 | tf_op jit(solution)/shard_map/ppermute | solution.py:288
  19.0 5.7 %collective-permute-done.3.refs_2_ = bf16[2,512,128]{2,1,0:T(8,128)(2,1)S(1)} collective-permute-done((bf16[2,512,128]{2,1,0:T(8,128)(2,1)S(1)}, bf16[2,512,128]{2,1,0:T(8,128)(2,1)S(1)}, u32[]{:S(2)}, u32[]{:S(2)}) %collective-permute-start.3) | collective-permute-done | bytes 262176 | tf_op jit(solution)/shard_map/ppermute | solution.py:289
  24.6 0.1 pair.1.refs_5_
  24.7 1.9 %collective-permute-start.4 = (bf16[3,2,512,128]{3,2,1,0:T(8,128)(2,1)S(1)}, bf16[3,2,512,128]{3,2,1,0:T(8,128)(2,1)S(1)}, u32[]{:S(2)}, u32[]{:S(2)}) collective-permute-start(bf16[3,2,512,128]{3,2,1,0:T(8,128)(2,1)S(1)} %pair.1.refs_5_), channel_id=1, source_target_pairs={{0,8},{8,0},{1,9},{9,1},{2,10},{10,2},{3,11},{11,3},{4,12},{12,4},... | collective-permute-start | bytes 2359304 | tf_op jit(solution)/shard_map/ppermute | solution.py:296
  26.6 0.0 copy-done.1
  26.6 0.8 spread.1
  27.4 14.6 %all-to-all-start = ((bf16[64,16,128]{2,1,0:T(8,128)(2,1)}), bf16[64,16,128]{2,1,0:T(8,128)(2,1)S(1)}, u32[]{:S(2)}, u32[]{:S(2)}) async-start(bf16[64,16,128]{2,1,0:T(8,128)(2,1)} %spread.1), calls=%async_computation | async-start | bytes 524288 | tf_op jit(solution)/shard_map/all_to_all | solution.py:292
  42.0 1.9 %collective-permute-start.1 = (bf16[2,512,128]{2,1,0:T(8,128)(2,1)S(1)}, bf16[2,512,128]{2,1,0:T(8,128)(2,1)S(1)}, u32[]{:S(2)}, u32[]{:S(2)}) collective-permute-start(bf16[2,512,128]{2,1,0:T(8,128)(2,1)S(1)} %collective-permute-done.refs_1_), channel_id=1, source_target_pairs={{0,128},{128,256},{256,384},{384,0},{1,129},{129,257},{257,385},{3... | collective-permute-start | bytes 786440 | tf_op jit(solution)/shard_map/ppermute | solution.py:290
  43.9 14.7 %collective-permute-done.1.refs_5_ = bf16[2,512,128]{2,1,0:T(8,128)(2,1)S(1)} collective-permute-done((bf16[2,512,128]{2,1,0:T(8,128)(2,1)S(1)}, bf16[2,512,128]{2,1,0:T(8,128)(2,1)S(1)}, u32[]{:S(2)}, u32[]{:S(2)}) %collective-permute-start.1) | collective-permute-done | bytes 262176 | tf_op jit(solution)/shard_map/ppermute | solution.py:290
  58.6 1.9 %collective-permute-start.2 = (bf16[2,512,128]{2,1,0:T(8,128)(2,1)S(1)}, bf16[2,512,128]{2,1,0:T(8,128)(2,1)S(1)}, u32[]{:S(2)}, u32[]{:S(2)}) collective-permute-start(bf16[2,512,128]{2,1,0:T(8,128)(2,1)S(1)} %collective-permute-done.1.refs_5_), channel_id=1, source_target_pairs={{0,8},{8,0},{1,9},{9,1},{2,10},{10,2},{3,11},{11,3},{4,12},{12,4},... | collective-permute-start | bytes 786440 | tf_op jit(solution)/shard_map/ppermute | solution.py:297
  60.6 0.0 copy-start.3
  60.6 0.0 copy-start.4
  60.6 0.1 pad_add_fusion.place_ref
  60.7 0.6 copy-done.3
  61.3 0.0 copy-done.4
  61.3 0.8 prep.1
  62.1 0.0 all-to-all-done
  62.1 3.0 %attend.4.refs_6_ = f32[136,1024]{1,0:T(8,128)S(1)} custom-call(bf16[1024,128]{1,0:T(8,128)(2,1)S(1)} %bitcast.8, s32[8,128]{1,0:T(8,128)S(1)} %get-tuple-element.8.refs_1_, s32[8,16,128]{2,1,0:T(8,128)S(1)} %get-tuple-element.9.refs_2_, s32[8,128]{1,0:T(8,128)S(1)} %get-tuple-element.10.refs_3_, bf16[1024,128]{1,0:T(8,128)(2,1)S(1)} %get-tuple-element.11.refs_4_, ...), custom_call_target="tpu_custom_call" | custom-call | flops 805306368 | bytes 1048576 | tf_op jit(solution)/shard_map/attend/pallas_call | solution.py:215
  65.1 0.0 collective-permute-done.4.refs_5_
  65.1 3.1 %attend.5.refs_6_ = f32[136,1024]{1,0:T(8,128)S(1)} custom-call(bf16[1024,128]{1,0:T(8,128)(2,1)S(1)} %bitcast.9, s32[8,128]{1,0:T(8,128)S(1)} %get-tuple-element.8.refs_1_, s32[8,16,128]{2,1,0:T(8,128)S(1)} %get-tuple-element.9.refs_2_, s32[8,128]{1,0:T(8,128)S(1)} %get-tuple-element.10.refs_3_, ...), custom_call_target="tpu_custom_call", output_to_operand_aliasing={{}: (6, {})} | custom-call | flops 805306368 | bytes 1048576 | tf_op jit(solution)/shard_map/attend/pallas_call | solution.py:215
  68.2 1.2 %attend.6.refs_6_ = f32[136,1024]{1,0:T(8,128)S(1)} custom-call(bf16[1024,128]{1,0:T(8,128)(2,1)S(1)} %bitcast.10, s32[8,128]{1,0:T(8,128)S(1)} %get-tuple-element.8.refs_1_, s32[8,16,128]{2,1,0:T(8,128)S(1)} %get-tuple-element.9.refs_2_, s32[8,128]{1,0:T(8,128)S(1)} %get-tuple-element.10.refs_3_, ...), custom_call_target="tpu_custom_call", output_to_operand_aliasing={{}: (6, {})} | custom-call | flops 268435456 | bytes 1048576 | tf_op jit(solution)/shard_map/attend/pallas_call | solution.py:215
  69.4 0.0 collective-permute-done.2.refs_5_
  69.4 1.2 %attend.7 = s32[640,128]{1,0:T(8,128)S(1)} custom-call(bf16[1024,128]{1,0:T(8,128)(2,1)S(1)} %bitcast.11, s32[8,128]{1,0:T(8,128)S(1)} %get-tuple-element.8.refs_1_, s32[8,16,128]{2,1,0:T(8,128)S(1)} %get-tuple-element.9.refs_2_, s32[8,128]{1,0:T(8,128)S(1)} %get-tuple-element.10.refs_3_, bf16[1024,128]{1,0:T(8,128)(2,1)S(1)} %get-tuple-element.11.refs_4_, ...), custom_call_target="tpu_custom_call" | custom-call | flops 268435456 | bytes 1048576 | tf_op jit(solution)/shard_map/attend/pallas_call | solution.py:215
  70.7 25.8 %all_to_all.10 = s32[64,1,1280]{2,1,0:T(1,128)S(1)} all-to-all(s32[64,1,1280]{2,1,0:T(1,128)S(1)} %bitcast.13), channel_id=1, replica_groups=mesh['y1'=2,'y0'=2,'z1'=4,'z0'=2,'core'=2,'x'=4,'yl'=2] {'z1','z0','x','..., dimensions={0} | all-to-all | bytes 655360 | tf_op jit(solution)/shard_map/all_to_all | solution.py:305
  96.4 1.6 %combine.1 = (bf16[2,8192]{1,0:T(2,128)(2,1)}, f32[8,16]{1,0:T(8,128)}) custom-call(s32[4]{0:T(128)S(1)} %pad_add_fusion.place_ref, s32[640,128]{1,0:T(8,128)S(1)} %bitcast.12), custom_call_target="tpu_custom_call" | custom-call | tf_op jit(solution)/shard_map/combine/pallas_call | solution.py:267
  (1 shorter events, 0.0 us)
Async XLA Ops:
  0.6 0.9 copy-start
  1.6 0.7 copy-start.2
  2.3 24.3 %copy-start.1 = (bf16[2,8192]{1,0:T(2,128)(2,1)S(1)}, bf16[2,8192]{1,0:T(2,128)(2,1)}, u32[]{:S(2)}) copy-start(bf16[2,8192]{1,0:T(2,128)(2,1)} %q_ref.1) | copy-start | bytes 98308
  2.3 16.7 %collective-permute-start = (bf16[2,512,128]{2,1,0:T(8,128)(2,1)S(1)}, bf16[2,512,128]{2,1,0:T(8,128)(2,1)S(1)}, u32[]{:S(2)}, u32[]{:S(2)}) collective-permute-start(bf16[2,512,128]{2,1,0:T(8,128)(2,1)S(1)} %join.1.refs_0_), channel_id=1, source_target_pairs={{0,128},{128,256},{256,384},{384,0},{1,129},{129,257},{257,385},{3... | collective-permute-start | bytes 786440 | tf_op jit(solution)/shard_map/ppermute | solution.py:288
  8.0 16.6 %collective-permute-start.3 = (bf16[2,512,128]{2,1,0:T(8,128)(2,1)S(1)}, bf16[2,512,128]{2,1,0:T(8,128)(2,1)S(1)}, u32[]{:S(2)}, u32[]{:S(2)}) collective-permute-start(bf16[2,512,128]{2,1,0:T(8,128)(2,1)S(1)} %join.1.refs_0_), channel_id=1, source_target_pairs={{0,384},{128,0},{256,128},{384,256},{1,385},{129,1},{257,129},{385... | collective-permute-start | bytes 786440 | tf_op jit(solution)/shard_map/ppermute | solution.py:289
  24.7 40.4 %collective-permute-start.4 = (bf16[3,2,512,128]{3,2,1,0:T(8,128)(2,1)S(1)}, bf16[3,2,512,128]{3,2,1,0:T(8,128)(2,1)S(1)}, u32[]{:S(2)}, u32[]{:S(2)}) collective-permute-start(bf16[3,2,512,128]{3,2,1,0:T(8,128)(2,1)S(1)} %pair.1.refs_5_), channel_id=1, source_target_pairs={{0,8},{8,0},{1,9},{9,1},{2,10},{10,2},{3,11},{11,3},{4,12},{12,4},... | collective-permute-start | bytes 2359304 | tf_op jit(solution)/shard_map/ppermute | solution.py:296
  27.4 34.7 %all-to-all-start = ((bf16[64,16,128]{2,1,0:T(8,128)(2,1)}), bf16[64,16,128]{2,1,0:T(8,128)(2,1)S(1)}, u32[]{:S(2)}, u32[]{:S(2)}) async-start(bf16[64,16,128]{2,1,0:T(8,128)(2,1)} %spread.1), calls=%async_computation | async-start | bytes 524288 | tf_op jit(solution)/shard_map/all_to_all | solution.py:292
  42.0 16.7 %collective-permute-start.1 = (bf16[2,512,128]{2,1,0:T(8,128)(2,1)S(1)}, bf16[2,512,128]{2,1,0:T(8,128)(2,1)S(1)}, u32[]{:S(2)}, u32[]{:S(2)}) collective-permute-start(bf16[2,512,128]{2,1,0:T(8,128)(2,1)S(1)} %collective-permute-done.refs_1_), channel_id=1, source_target_pairs={{0,128},{128,256},{256,384},{384,0},{1,129},{129,257},{257,385},{3... | collective-permute-start | bytes 786440 | tf_op jit(solution)/shard_map/ppermute | solution.py:290
  58.6 10.8 %collective-permute-start.2 = (bf16[2,512,128]{2,1,0:T(8,128)(2,1)S(1)}, bf16[2,512,128]{2,1,0:T(8,128)(2,1)S(1)}, u32[]{:S(2)}, u32[]{:S(2)}) collective-permute-start(bf16[2,512,128]{2,1,0:T(8,128)(2,1)S(1)} %collective-permute-done.1.refs_5_), channel_id=1, source_target_pairs={{0,8},{8,0},{1,9},{9,1},{2,10},{10,2},{3,11},{11,3},{4,12},{12,4},... | collective-permute-start | bytes 786440 | tf_op jit(solution)/shard_map/ppermute | solution.py:297
  60.6 0.7 copy-start.3
  60.6 0.7 copy-start.4

commit v4 on v3

--- a/solution.py
+++ b/solution.py
@@ -32,7 +32,9 @@
     qseg_ref[...] = qseg
     filled = jnp.zeros((8, 128), jnp.int32)
     for j in range(8):
-        shard = ((y + 4 - j // 2) % 4) * 16 + z * 2 + (core if j % 2 == 0 else 1 - core)
+        side = core if j % 2 == 0 else 1 - core
+        step = j // 2
+        shard = ((y + 4 - step + 2 * step * side) % 4) * 16 + z * 2 + side
         filled = jnp.where(which == j, lens_ref[shard], filled)
         kseg = jnp.zeros((block, 128), jnp.int32)
         for i in range(block):
@@ -228,8 +230,8 @@
     )(*operands)
 
 
-def combine_kernel(place_ref, got_ref, out_ref, lse_ref, turned_ref, line_ref):
-    me = place_ref[0]
+def combine_kernel(got_ref, out_ref, lse_ref, turned_ref, line_ref):
+    me = lax.axis_index("x") * 2 + lax.axis_index("yl")
     lse = got_ref[pl.ds(8, 64, stride=SENT), :].astype(jnp.float32) * (1.0 / 65536.0)
     power = got_ref[pl.ds(9, 64, stride=SENT), :].astype(jnp.float32) - 15.0
     lse = lse.reshape(8, 8, 128)
@@ -261,8 +263,7 @@
     lse_ref[...] = table[:8, :16]
 
 
-def combine(place, got):
-    smem = pl.BlockSpec(memory_space=pltpu.SMEM)
+def combine(got):
     vmem = pl.BlockSpec(memory_space=pltpu.VMEM)
     return pl.pallas_call(
         combine_kernel,
@@ -270,12 +271,12 @@
             jax.ShapeDtypeStruct((2, 8192), jnp.bfloat16),
             jax.ShapeDtypeStruct((8, 16), jnp.float32),
         ),
-        in_specs=[smem, vmem],
+        in_specs=[vmem],
         out_specs=(vmem, vmem),
         scratch_shapes=[pltpu.VMEM((128, 128), jnp.float32), pltpu.VMEM((8, 128), jnp.float32)],
         compiler_params=pltpu.CompilerParams(vmem_limit_bytes=8 << 20),
         name="combine",
-    )(place, got)
+    )(got)
 
 
 def shards_program(q_new, kv_new, kv_cache, cache_lens, segment_ids):
@@ -284,10 +285,11 @@
     swap = [(0, 1), (1, 0)]
 
     own = join(kv_cache, kv_new)
-    turn = lambda by: [(i, (i + by) % 4) for i in range(4)]
-    one = lax.ppermute(own, ("y1", "y0"), turn(1))
-    three = lax.ppermute(own, ("y1", "y0"), turn(3))
-    two = lax.ppermute(one, ("y1", "y0"), turn(1))
+    turn = lambda by: [(i * 2 + c, (i + (4 - by if c else by)) % 4 * 2 + c) for i in range(4) for c in range(2)]
+    ring = ("y1", "y0", "core")
+    one = lax.ppermute(own, ring, turn(1))
+    three = lax.ppermute(own, ring, turn(3))
+    two = lax.ppermute(one, ring, turn(1))
     q = spread(q_new)
     q = lax.all_to_all(q, ROUTE, split_axis=0, concat_axis=0, tiled=True)
     q = q.reshape(1024, HEAD)
@@ -303,7 +305,7 @@
         state = attend(flat, q, prepared, [chunk[j] for j in shards], state, final=final)
     sent = state.reshape(64, 1, SENT * 128)
     got = lax.all_to_all(sent, ROUTE, split_axis=0, concat_axis=0, tiled=True)
-    out, lse = combine(place, got.reshape(64 * SENT, 128))
+    out, lse = combine(got.reshape(64 * SENT, 128))
     return out, lse.T
 
 

time: 98.5 us -> 90.6 us (0.920)
  waiting for transfers between devices: 27.5 us -> 14.3 us
  starting transfers between devices: 29.8 us -> 34.2 us
  blocking collectives: 25.8 us -> 27.2 us
    ppermute x3, waiting for transfers between devices: 27.5 us -> 14.3 us  [the longest x1 9.16 us: shards_program(): one = lax.ppermute(own, ring, turn(1))]
    ppermute x3, starting transfers between devices: 11.4 us -> 13.6 us  [the longest x1 5.71 us: shards_program(): one = lax.ppermute(own, ring, turn(1))]
    ppermute x1, starting transfers between devices: 1.91 us -> 3.4 us  [shards_program(): sent1 = lax.ppermute(two, 'core', swap)]
    all_to_all x1, blocking collectives: 25.8 us -> 27.2 us  [shards_program(): got = lax.all_to_all(sent, ROUTE, split_axis=0, concat_axis=0, tiled=True)]
  transfers between devices with their start and end apart: 6 -> 6, of which waited for: 3 -> 2; matrix products, arithmetic and copies ran while one was open for 0% -> 0% of each run, Pallas kernels for 9% -> 10%
where the time goes in v4:
time: 90.6 us; the launch traced here: 90.1 us
  starting transfers between devices  34.2 us (38%)
  blocking collectives  27.2 us (30%)
  waiting for transfers between devices  14.3 us (16%)
  Pallas kernels  11.3 us (12%)
  local copies, waits for them, and re-layouts  2.24 us (2%)
    all_to_all x1, blocking collectives, shards_program(): got = lax.all_to_all(sent, ROUTE, split_axis=0, concat_axis=0, tiled=True)  27.2 us
    all_to_all x1, starting transfers between devices, shards_program(): q = lax.all_to_all(q, ROUTE, split_axis=0, concat_axis=0, tiled=True)  15.2 us
    ppermute x1, waiting for transfers between devices, shards_program(): one = lax.ppermute(own, ring, turn(1))  9.16 us
    pallas_call x4, Pallas kernels, attend(): pl.pallas_call(functools.partial(attend_kernel, tuple(shards), len(chunks...  8.51 us
    ppermute x1, starting transfers between devices, shards_program(): one = lax.ppermute(own, ring, turn(1))  5.71 us
    ppermute x1, waiting for transfers between devices, shards_program(): two = lax.ppermute(one, ring, turn(1))  5.15 us
    ppermute x1, starting transfers between devices, shards_program(): two = lax.ppermute(one, ring, turn(1))  4.1 us
    ppermute x1, starting transfers between devices, shards_program(): three = lax.ppermute(own, ring, turn(3))  3.8 us
  transfers between devices with their start and end apart: 6, of which 2 were waited for; matrix products, arithmetic and copies ran while one was open for 0% of the time, Pallas kernels for 10%

profile of v4, /device:TPU:16, one launch (start us, length us, event | category | flops | bytes accessed | tf_op | source)
XLA Modules:
  0.0 90.1 jit_solution(10422657038473906236)
XLA Ops:
  0.6 0.0 copy-start
  0.6 0.9 %copy-done = bf16[2,496,128]{2,1,0:T(8,128)(2,1)S(1)} copy-done((bf16[2,496,128]{2,1,0:T(8,128)(2,1)S(1)}, bf16[2,496,128]{2,1,0:T(8,128)(2,1)}, u32[]{:S(2)}) %copy-start) | copy-done | bytes 253976
  1.6 0.0 copy-start.2
  1.6 0.7 copy-done.2
  2.3 0.0 copy-start.1
  2.3 5.7 %collective-permute-start = (bf16[2,512,128]{2,1,0:T(8,128)(2,1)S(1)}, bf16[2,512,128]{2,1,0:T(8,128)(2,1)S(1)}, u32[]{:S(2)}, u32[]{:S(2)}) collective-permute-start(bf16[2,512,128]{2,1,0:T(8,128)(2,1)S(1)} %join.1.refs_0_), channel_id=1, source_target_pairs={{0,128},{8,392},{128,256},{136,8},{256,384},{264,136},{384,0},{392... | collective-permute-start | bytes 786440 | tf_op jit(solution)/shard_map/ppermute | solution.py:290
  8.0 3.8 %collective-permute-start.3 = (bf16[2,512,128]{2,1,0:T(8,128)(2,1)S(1)}, bf16[2,512,128]{2,1,0:T(8,128)(2,1)S(1)}, u32[]{:S(2)}, u32[]{:S(2)}) collective-permute-start(bf16[2,512,128]{2,1,0:T(8,128)(2,1)S(1)} %join.1.refs_0_), channel_id=1, source_target_pairs={{0,384},{8,136},{128,0},{136,264},{256,128},{264,392},{384,256},{3... | collective-permute-start | bytes 786440 | tf_op jit(solution)/shard_map/ppermute | solution.py:291
  11.8 9.2 %collective-permute-done.refs_1_ = bf16[2,512,128]{2,1,0:T(8,128)(2,1)S(1)} collective-permute-done((bf16[2,512,128]{2,1,0:T(8,128)(2,1)S(1)}, bf16[2,512,128]{2,1,0:T(8,128)(2,1)S(1)}, u32[]{:S(2)}, u32[]{:S(2)}) %collective-permute-start) | collective-permute-done | bytes 262176 | tf_op jit(solution)/shard_map/ppermute | solution.py:290
  21.0 0.0 collective-permute-done.3.refs_2_
  21.0 0.1 pair.1.refs_5_
  21.1 2.0 %collective-permute-start.4 = (bf16[3,2,512,128]{3,2,1,0:T(8,128)(2,1)S(1)}, bf16[3,2,512,128]{3,2,1,0:T(8,128)(2,1)S(1)}, u32[]{:S(2)}, u32[]{:S(2)}) collective-permute-start(bf16[3,2,512,128]{3,2,1,0:T(8,128)(2,1)S(1)} %pair.1.refs_5_), channel_id=1, source_target_pairs={{0,8},{8,0},{1,9},{9,1},{2,10},{10,2},{3,11},{11,3},{4,12},{12,4},... | collective-permute-start | bytes 2359304 | tf_op jit(solution)/shard_map/ppermute | solution.py:298
  23.1 0.0 copy-done.1
  23.1 0.8 spread.1
  23.8 15.2 %all-to-all-start = ((bf16[64,16,128]{2,1,0:T(8,128)(2,1)}), bf16[64,16,128]{2,1,0:T(8,128)(2,1)S(1)}, u32[]{:S(2)}, u32[]{:S(2)}) async-start(bf16[64,16,128]{2,1,0:T(8,128)(2,1)} %spread.1), calls=%async_computation | async-start | bytes 524288 | tf_op jit(solution)/shard_map/all_to_all | solution.py:294
  39.1 4.1 %collective-permute-start.1 = (bf16[2,512,128]{2,1,0:T(8,128)(2,1)S(1)}, bf16[2,512,128]{2,1,0:T(8,128)(2,1)S(1)}, u32[]{:S(2)}, u32[]{:S(2)}) collective-permute-start(bf16[2,512,128]{2,1,0:T(8,128)(2,1)S(1)} %collective-permute-done.refs_1_), channel_id=1, source_target_pairs={{0,128},{8,392},{128,256},{136,8},{256,384},{264,136},{384,0},{392... | collective-permute-start | bytes 786440 | tf_op jit(solution)/shard_map/ppermute | solution.py:292
  43.2 5.1 %collective-permute-done.1.refs_5_ = bf16[2,512,128]{2,1,0:T(8,128)(2,1)S(1)} collective-permute-done((bf16[2,512,128]{2,1,0:T(8,128)(2,1)S(1)}, bf16[2,512,128]{2,1,0:T(8,128)(2,1)S(1)}, u32[]{:S(2)}, u32[]{:S(2)}) %collective-permute-start.1) | collective-permute-done | bytes 262176 | tf_op jit(solution)/shard_map/ppermute | solution.py:292
  48.3 3.4 %collective-permute-start.2 = (bf16[2,512,128]{2,1,0:T(8,128)(2,1)S(1)}, bf16[2,512,128]{2,1,0:T(8,128)(2,1)S(1)}, u32[]{:S(2)}, u32[]{:S(2)}) collective-permute-start(bf16[2,512,128]{2,1,0:T(8,128)(2,1)S(1)} %collective-permute-done.1.refs_5_), channel_id=1, source_target_pairs={{0,8},{8,0},{1,9},{9,1},{2,10},{10,2},{3,11},{11,3},{4,12},{12,4},... | collective-permute-start | bytes 786440 | tf_op jit(solution)/shard_map/ppermute | solution.py:299
  51.7 0.0 copy-start.3
  51.8 0.0 copy-start.4
  51.8 0.1 pad_add_fusion.place_ref
  51.8 0.6 copy-done.3
  52.4 0.0 copy-done.4
  52.4 0.8 prep.1
  53.3 0.0 all-to-all-done
  53.3 3.0 %attend.4.refs_6_ = f32[136,1024]{1,0:T(8,128)S(1)} custom-call(bf16[1024,128]{1,0:T(8,128)(2,1)S(1)} %bitcast.8, s32[8,128]{1,0:T(8,128)S(1)} %get-tuple-element.8.refs_1_, s32[8,16,128]{2,1,0:T(8,128)S(1)} %get-tuple-element.9.refs_2_, s32[8,128]{1,0:T(8,128)S(1)} %get-tuple-element.10.refs_3_, bf16[1024,128]{1,0:T(8,128)(2,1)S(1)} %get-tuple-element.11.refs_4_, ...), custom_call_target="tpu_custom_call" | custom-call | flops 805306368 | bytes 1048576 | tf_op jit(solution)/shard_map/attend/pallas_call | solution.py:217
  56.3 0.0 collective-permute-done.4.refs_5_
  56.3 3.1 %attend.5.refs_6_ = f32[136,1024]{1,0:T(8,128)S(1)} custom-call(bf16[1024,128]{1,0:T(8,128)(2,1)S(1)} %bitcast.9, s32[8,128]{1,0:T(8,128)S(1)} %get-tuple-element.8.refs_1_, s32[8,16,128]{2,1,0:T(8,128)S(1)} %get-tuple-element.9.refs_2_, s32[8,128]{1,0:T(8,128)S(1)} %get-tuple-element.10.refs_3_, ...), custom_call_target="tpu_custom_call", output_to_operand_aliasing={{}: (6, {})} | custom-call | flops 805306368 | bytes 1048576 | tf_op jit(solution)/shard_map/attend/pallas_call | solution.py:217
  59.4 1.2 %attend.6.refs_6_ = f32[136,1024]{1,0:T(8,128)S(1)} custom-call(bf16[1024,128]{1,0:T(8,128)(2,1)S(1)} %bitcast.10, s32[8,128]{1,0:T(8,128)S(1)} %get-tuple-element.8.refs_1_, s32[8,16,128]{2,1,0:T(8,128)S(1)} %get-tuple-element.9.refs_2_, s32[8,128]{1,0:T(8,128)S(1)} %get-tuple-element.10.refs_3_, ...), custom_call_target="tpu_custom_call", output_to_operand_aliasing={{}: (6, {})} | custom-call | flops 268435456 | bytes 1048576 | tf_op jit(solution)/shard_map/attend/pallas_call | solution.py:217
  60.6 0.0 collective-permute-done.2.refs_5_
  60.6 1.2 %attend.7 = s32[640,128]{1,0:T(8,128)S(1)} custom-call(bf16[1024,128]{1,0:T(8,128)(2,1)S(1)} %bitcast.11, s32[8,128]{1,0:T(8,128)S(1)} %get-tuple-element.8.refs_1_, s32[8,16,128]{2,1,0:T(8,128)S(1)} %get-tuple-element.9.refs_2_, s32[8,128]{1,0:T(8,128)S(1)} %get-tuple-element.10.refs_3_, bf16[1024,128]{1,0:T(8,128)(2,1)S(1)} %get-tuple-element.11.refs_4_, ...), custom_call_target="tpu_custom_call" | custom-call | flops 268435456 | bytes 1048576 | tf_op jit(solution)/shard_map/attend/pallas_call | solution.py:217
  61.8 27.2 %all_to_all.10 = s32[64,1,1280]{2,1,0:T(1,128)S(1)} all-to-all(s32[64,1,1280]{2,1,0:T(1,128)S(1)} %bitcast.13), channel_id=1, replica_groups=mesh['y1'=2,'y0'=2,'z1'=4,'z0'=2,'core'=2,'x'=4,'yl'=2] {'z1','z0','x','..., dimensions={0} | all-to-all | bytes 655360 | tf_op jit(solution)/shard_map/all_to_all | solution.py:307
  89.0 1.1 %combine.1 = (bf16[2,8192]{1,0:T(2,128)(2,1)}, f32[8,16]{1,0:T(8,128)}) custom-call(s32[640,128]{1,0:T(8,128)S(1)} %bitcast.12), custom_call_target="tpu_custom_call" | custom-call | tf_op jit(solution)/shard_map/combine/pallas_call | solution.py:268
  (1 shorter events, 0.0 us)
Async XLA Ops:
  0.6 0.9 %copy-start = (bf16[2,496,128]{2,1,0:T(8,128)(2,1)S(1)}, bf16[2,496,128]{2,1,0:T(8,128)(2,1)}, u32[]{:S(2)}) copy-start(bf16[2,496,128]{2,1,0:T(8,128)(2,1)} %cache_ref.1) | copy-start | bytes 761860
  1.6 0.7 copy-start.2
  2.3 20.8 %copy-start.1 = (bf16[2,8192]{1,0:T(2,128)(2,1)S(1)}, bf16[2,8192]{1,0:T(2,128)(2,1)}, u32[]{:S(2)}) copy-start(bf16[2,8192]{1,0:T(2,128)(2,1)} %q_ref.1) | copy-start | bytes 98308
  2.3 18.7 %collective-permute-start = (bf16[2,512,128]{2,1,0:T(8,128)(2,1)S(1)}, bf16[2,512,128]{2,1,0:T(8,128)(2,1)S(1)}, u32[]{:S(2)}, u32[]{:S(2)}) collective-permute-start(bf16[2,512,128]{2,1,0:T(8,128)(2,1)S(1)} %join.1.refs_0_), channel_id=1, source_target_pairs={{0,128},{8,392},{128,256},{136,8},{256,384},{264,136},{384,0},{392... | collective-permute-start | bytes 786440 | tf_op jit(solution)/shard_map/ppermute | solution.py:290
  8.0 13.0 %collective-permute-start.3 = (bf16[2,512,128]{2,1,0:T(8,128)(2,1)S(1)}, bf16[2,512,128]{2,1,0:T(8,128)(2,1)S(1)}, u32[]{:S(2)}, u32[]{:S(2)}) collective-permute-start(bf16[2,512,128]{2,1,0:T(8,128)(2,1)S(1)} %join.1.refs_0_), channel_id=1, source_target_pairs={{0,384},{8,136},{128,0},{136,264},{256,128},{264,392},{384,256},{3... | collective-permute-start | bytes 786440 | tf_op jit(solution)/shard_map/ppermute | solution.py:291
  21.1 35.2 %collective-permute-start.4 = (bf16[3,2,512,128]{3,2,1,0:T(8,128)(2,1)S(1)}, bf16[3,2,512,128]{3,2,1,0:T(8,128)(2,1)S(1)}, u32[]{:S(2)}, u32[]{:S(2)}) collective-permute-start(bf16[3,2,512,128]{3,2,1,0:T(8,128)(2,1)S(1)} %pair.1.refs_5_), channel_id=1, source_target_pairs={{0,8},{8,0},{1,9},{9,1},{2,10},{10,2},{3,11},{11,3},{4,12},{12,4},... | collective-permute-start | bytes 2359304 | tf_op jit(solution)/shard_map/ppermute | solution.py:298
  23.8 29.4 %all-to-all-start = ((bf16[64,16,128]{2,1,0:T(8,128)(2,1)}), bf16[64,16,128]{2,1,0:T(8,128)(2,1)S(1)}, u32[]{:S(2)}, u32[]{:S(2)}) async-start(bf16[64,16,128]{2,1,0:T(8,128)(2,1)} %spread.1), calls=%async_computation | async-start | bytes 524288 | tf_op jit(solution)/shard_map/all_to_all | solution.py:294
  39.1 9.3 %collective-permute-start.1 = (bf16[2,512,128]{2,1,0:T(8,128)(2,1)S(1)}, bf16[2,512,128]{2,1,0:T(8,128)(2,1)S(1)}, u32[]{:S(2)}, u32[]{:S(2)}) collective-permute-start(bf16[2,512,128]{2,1,0:T(8,128)(2,1)S(1)} %collective-permute-done.refs_1_), channel_id=1, source_target_pairs={{0,128},{8,392},{128,256},{136,8},{256,384},{264,136},{384,0},{392... | collective-permute-start | bytes 786440 | tf_op jit(solution)/shard_map/ppermute | solution.py:292
  48.3 12.3 %collective-permute-start.2 = (bf16[2,512,128]{2,1,0:T(8,128)(2,1)S(1)}, bf16[2,512,128]{2,1,0:T(8,128)(2,1)S(1)}, u32[]{:S(2)}, u32[]{:S(2)}) collective-permute-start(bf16[2,512,128]{2,1,0:T(8,128)(2,1)S(1)} %collective-permute-done.1.refs_5_), channel_id=1, source_target_pairs={{0,8},{8,0},{1,9},{9,1},{2,10},{10,2},{3,11},{11,3},{4,12},{12,4},... | collective-permute-start | bytes 786440 | tf_op jit(solution)/shard_map/ppermute | solution.py:299
  51.7 0.7 copy-start.3
  51.8 0.7 copy-start.4

commit v5 on v4

--- a/solution.py
+++ b/solution.py
@@ -18,9 +18,11 @@
 ROUTE = ("z1", "z0", "x", "yl")
 
 
-def prep_kernel(lens_ref, ids_ref, place_ref, filled_ref, kseg_ref, qseg_ref, pick_ref):
+def prep_kernel(lens_ref, ids_ref, filled_ref, kseg_ref, qseg_ref, pick_ref):
     block = pick_ref.shape[0] // 64
-    y, z, core = place_ref[1], place_ref[2], place_ref[3]
+    y = lax.axis_index("y1") * 2 + lax.axis_index("y0")
+    z = lax.axis_index("z1") * 2 + lax.axis_index("z0")
+    core = lax.axis_index("core")
     row = lax.broadcasted_iota(jnp.int32, (block, 128), 0)
     lane = lax.broadcasted_iota(jnp.int32, (8, 128), 1)
     which = lax.broadcasted_iota(jnp.int32, (8, 128), 0)
@@ -46,7 +48,7 @@
     pick_ref[...] = jnp.where(picked, 1.0, 0.0).astype(jnp.bfloat16)
 
 
-def prep(lens, ids, place):
+def prep(lens, ids):
     smem = pl.BlockSpec(memory_space=pltpu.SMEM)
     vmem = pl.BlockSpec(memory_space=pltpu.VMEM)
     return pl.pallas_call(
@@ -57,11 +59,11 @@
             jax.ShapeDtypeStruct((8, 128), jnp.int32),
             jax.ShapeDtypeStruct((1024, 128), jnp.bfloat16),
         ),
-        in_specs=[smem, smem, smem],
+        in_specs=[smem, smem],
         out_specs=(vmem, vmem, vmem, vmem),
         compiler_params=pltpu.CompilerParams(vmem_limit_bytes=4 << 20),
         name="prep",
-    )(lens, ids, place)
+    )(lens, ids)
 
 
 def join_kernel(cache_ref, new_ref, out_ref):
@@ -132,7 +134,7 @@
     state_ref = rest[0] if has_state else None
     out_ref, turned_ref, hide_ref = rest[-3:]
     rows = q_ref.shape[0]
-    tile = 256
+    tile = 256 if final else 512
     scale = HEAD**-0.5
     factor = scale * math.log2(math.e)
     steps = [(part, which) for part in range(rows // tile) for which in range(len(shards))]
@@ -280,8 +282,6 @@
 
 
 def shards_program(q_new, kv_new, kv_cache, cache_lens, segment_ids):
-    y1, y0, z1, z0, core = (lax.axis_index(name) for name in CTX)
-    place = jnp.stack([lax.axis_index(TP), y1 * 2 + y0, z1 * 2 + z0, core]).astype(jnp.int32)
     swap = [(0, 1), (1, 0)]
 
     own = join(kv_cache, kv_new)
@@ -293,7 +293,7 @@
     q = spread(q_new)
     q = lax.all_to_all(q, ROUTE, split_axis=0, concat_axis=0, tiled=True)
     q = q.reshape(1024, HEAD)
-    prepared = prep(cache_lens, segment_ids, place)
+    prepared = prep(cache_lens, segment_ids)
     both0 = pair(own, one, three)
     sent0 = lax.ppermute(both0, "core", swap)
     sent1 = lax.ppermute(two, "core", swap)

time: 90.6 us -> 89.4 us (0.987)
  transfers between devices with their start and end apart: 6 -> 6, of which waited for: 2 -> 3; matrix products, arithmetic and copies ran while one was open for 0% -> 0% of each run, Pallas kernels for 10% -> 9%
where the time goes in v5:
time: 89.4 us; the launch traced here: 88.9 us
  starting transfers between devices  34.3 us (38%)
  blocking collectives  27 us (30%)
  waiting for transfers between devices  14.5 us (16%)
  Pallas kernels  10.6 us (12%)
  local copies, waits for them, and re-layouts  1.65 us (2%)
    all_to_all x1, blocking collectives, shards_program(): got = lax.all_to_all(sent, ROUTE, split_axis=0, concat_axis=0, tiled=True)  27 us
    all_to_all x1, starting transfers between devices, shards_program(): q = lax.all_to_all(q, ROUTE, split_axis=0, concat_axis=0, tiled=True)  15.3 us
    ppermute x1, waiting for transfers between devices, shards_program(): one = lax.ppermute(own, ring, turn(1))  9.16 us
    pallas_call x4, Pallas kernels, attend(): pl.pallas_call(functools.partial(attend_kernel, tuple(shards), len(chunks...  7.81 us
    ppermute x1, starting transfers between devices, shards_program(): one = lax.ppermute(own, ring, turn(1))  5.71 us
    ppermute x1, waiting for transfers between devices, shards_program(): two = lax.ppermute(one, ring, turn(1))  5.16 us
    ppermute x1, starting transfers between devices, shards_program(): two = lax.ppermute(one, ring, turn(1))  4.1 us
    ppermute x1, starting transfers between devices, shards_program(): three = lax.ppermute(own, ring, turn(3))  3.8 us
  transfers between devices with their start and end apart: 6, of which 3 were waited for; matrix products, arithmetic and copies ran while one was open for 0% of the time, Pallas kernels for 9%

profile of v5, /device:TPU:16, one launch (start us, length us, event | category | flops | bytes accessed | tf_op | source)
XLA Modules:
  0.0 88.9 jit_solution(3685674200405905902)
XLA Ops:
  0.6 0.0 copy-start
  0.6 0.9 %copy-done = bf16[2,496,128]{2,1,0:T(8,128)(2,1)S(1)} copy-done((bf16[2,496,128]{2,1,0:T(8,128)(2,1)S(1)}, bf16[2,496,128]{2,1,0:T(8,128)(2,1)}, u32[]{:S(2)}) %copy-start) | copy-done | bytes 253976
  1.6 0.0 copy-start.2
  1.6 0.7 copy-done.2
  2.3 0.0 copy-start.1
  2.3 5.7 %collective-permute-start = (bf16[2,512,128]{2,1,0:T(8,128)(2,1)S(1)}, bf16[2,512,128]{2,1,0:T(8,128)(2,1)S(1)}, u32[]{:S(2)}, u32[]{:S(2)}) collective-permute-start(bf16[2,512,128]{2,1,0:T(8,128)(2,1)S(1)} %join.1.refs_0_), channel_id=1, source_target_pairs={{0,128},{8,392},{128,256},{136,8},{256,384},{264,136},{384,0},{392... | collective-permute-start | bytes 786440 | tf_op jit(solution)/shard_map/ppermute | solution.py:290
  8.0 3.8 %collective-permute-start.3 = (bf16[2,512,128]{2,1,0:T(8,128)(2,1)S(1)}, bf16[2,512,128]{2,1,0:T(8,128)(2,1)S(1)}, u32[]{:S(2)}, u32[]{:S(2)}) collective-permute-start(bf16[2,512,128]{2,1,0:T(8,128)(2,1)S(1)} %join.1.refs_0_), channel_id=1, source_target_pairs={{0,384},{8,136},{128,0},{136,264},{256,128},{264,392},{384,256},{3... | collective-permute-start | bytes 786440 | tf_op jit(solution)/shard_map/ppermute | solution.py:291
  11.8 9.2 %collective-permute-done.refs_1_ = bf16[2,512,128]{2,1,0:T(8,128)(2,1)S(1)} collective-permute-done((bf16[2,512,128]{2,1,0:T(8,128)(2,1)S(1)}, bf16[2,512,128]{2,1,0:T(8,128)(2,1)S(1)}, u32[]{:S(2)}, u32[]{:S(2)}) %collective-permute-start) | collective-permute-done | bytes 262176 | tf_op jit(solution)/shard_map/ppermute | solution.py:290
  21.0 0.0 collective-permute-done.3.refs_2_
  21.0 0.1 pair.1.refs_5_
  21.1 2.0 %collective-permute-start.4 = (bf16[3,2,512,128]{3,2,1,0:T(8,128)(2,1)S(1)}, bf16[3,2,512,128]{3,2,1,0:T(8,128)(2,1)S(1)}, u32[]{:S(2)}, u32[]{:S(2)}) collective-permute-start(bf16[3,2,512,128]{3,2,1,0:T(8,128)(2,1)S(1)} %pair.1.refs_5_), channel_id=1, source_target_pairs={{0,8},{8,0},{1,9},{9,1},{2,10},{10,2},{3,11},{11,3},{4,12},{12,4},... | collective-permute-start | bytes 2359304 | tf_op jit(solution)/shard_map/ppermute | solution.py:298
  23.1 0.0 copy-done.1
  23.1 0.8 spread.1
  23.8 0.0 copy-start.3
  23.9 0.0 copy-start.4
  23.9 15.3 %all-to-all-start = ((bf16[64,16,128]{2,1,0:T(8,128)(2,1)}), bf16[64,16,128]{2,1,0:T(8,128)(2,1)S(1)}, u32[]{:S(2)}, u32[]{:S(2)}) async-start(bf16[64,16,128]{2,1,0:T(8,128)(2,1)} %spread.1), calls=%async_computation | async-start | bytes 524288 | tf_op jit(solution)/shard_map/all_to_all | solution.py:294
  39.2 4.1 %collective-permute-start.1 = (bf16[2,512,128]{2,1,0:T(8,128)(2,1)S(1)}, bf16[2,512,128]{2,1,0:T(8,128)(2,1)S(1)}, u32[]{:S(2)}, u32[]{:S(2)}) collective-permute-start(bf16[2,512,128]{2,1,0:T(8,128)(2,1)S(1)} %collective-permute-done.refs_1_), channel_id=1, source_target_pairs={{0,128},{8,392},{128,256},{136,8},{256,384},{264,136},{384,0},{392... | collective-permute-start | bytes 786440 | tf_op jit(solution)/shard_map/ppermute | solution.py:292
  43.3 5.2 %collective-permute-done.1.refs_5_ = bf16[2,512,128]{2,1,0:T(8,128)(2,1)S(1)} collective-permute-done((bf16[2,512,128]{2,1,0:T(8,128)(2,1)S(1)}, bf16[2,512,128]{2,1,0:T(8,128)(2,1)S(1)}, u32[]{:S(2)}, u32[]{:S(2)}) %collective-permute-start.1) | collective-permute-done | bytes 262176 | tf_op jit(solution)/shard_map/ppermute | solution.py:292
  48.5 3.4 %collective-permute-start.2 = (bf16[2,512,128]{2,1,0:T(8,128)(2,1)S(1)}, bf16[2,512,128]{2,1,0:T(8,128)(2,1)S(1)}, u32[]{:S(2)}, u32[]{:S(2)}) collective-permute-start(bf16[2,512,128]{2,1,0:T(8,128)(2,1)S(1)} %collective-permute-done.1.refs_5_), channel_id=1, source_target_pairs={{0,8},{8,0},{1,9},{9,1},{2,10},{10,2},{3,11},{11,3},{4,12},{12,4},... | collective-permute-start | bytes 786440 | tf_op jit(solution)/shard_map/ppermute | solution.py:299
  51.9 0.0 copy-done.3
  51.9 0.0 copy-done.4
  51.9 0.8 prep.1
  52.7 0.2 all-to-all-done
  53.0 2.6 %attend.4.refs_6_ = f32[136,1024]{1,0:T(8,128)S(1)} custom-call(bf16[1024,128]{1,0:T(8,128)(2,1)S(1)} %bitcast.4, s32[8,128]{1,0:T(8,128)S(1)} %get-tuple-element.8.refs_1_, s32[8,16,128]{2,1,0:T(8,128)S(1)} %get-tuple-element.9.refs_2_, s32[8,128]{1,0:T(8,128)S(1)} %get-tuple-element.10.refs_3_, bf16[1024,128]{1,0:T(8,128)(2,1)S(1)} %get-tuple-element.11.refs_4_, ...), custom_call_target="tpu_custom_call" | custom-call | flops 805306368 | bytes 1048576 | tf_op jit(solution)/shard_map/attend/pallas_call | solution.py:219
  55.6 0.0 collective-permute-done.4.refs_5_
  55.6 2.8 %attend.5.refs_6_ = f32[136,1024]{1,0:T(8,128)S(1)} custom-call(bf16[1024,128]{1,0:T(8,128)(2,1)S(1)} %bitcast.5, s32[8,128]{1,0:T(8,128)S(1)} %get-tuple-element.8.refs_1_, s32[8,16,128]{2,1,0:T(8,128)S(1)} %get-tuple-element.9.refs_2_, s32[8,128]{1,0:T(8,128)S(1)} %get-tuple-element.10.refs_3_, ...), custom_call_target="tpu_custom_call", output_to_operand_aliasing={{}: (6, {})} | custom-call | flops 805306368 | bytes 1048576 | tf_op jit(solution)/shard_map/attend/pallas_call | solution.py:219
  58.4 1.1 %attend.6.refs_6_ = f32[136,1024]{1,0:T(8,128)S(1)} custom-call(bf16[1024,128]{1,0:T(8,128)(2,1)S(1)} %bitcast.6, s32[8,128]{1,0:T(8,128)S(1)} %get-tuple-element.8.refs_1_, s32[8,16,128]{2,1,0:T(8,128)S(1)} %get-tuple-element.9.refs_2_, s32[8,128]{1,0:T(8,128)S(1)} %get-tuple-element.10.refs_3_, ...), custom_call_target="tpu_custom_call", output_to_operand_aliasing={{}: (6, {})} | custom-call | flops 268435456 | bytes 1048576 | tf_op jit(solution)/shard_map/attend/pallas_call | solution.py:219
  59.6 0.0 collective-permute-done.2.refs_5_
  59.6 1.2 %attend.7 = s32[640,128]{1,0:T(8,128)S(1)} custom-call(bf16[1024,128]{1,0:T(8,128)(2,1)S(1)} %bitcast.7, s32[8,128]{1,0:T(8,128)S(1)} %get-tuple-element.8.refs_1_, s32[8,16,128]{2,1,0:T(8,128)S(1)} %get-tuple-element.9.refs_2_, s32[8,128]{1,0:T(8,128)S(1)} %get-tuple-element.10.refs_3_, bf16[1024,128]{1,0:T(8,128)(2,1)S(1)} %get-tuple-element.11.refs_4_, ...), custom_call_target="tpu_custom_call" | custom-call | flops 268435456 | bytes 1048576 | tf_op jit(solution)/shard_map/attend/pallas_call | solution.py:219
  60.8 27.0 %all_to_all.10 = s32[64,1,1280]{2,1,0:T(1,128)S(1)} all-to-all(s32[64,1,1280]{2,1,0:T(1,128)S(1)} %bitcast.9), channel_id=1, replica_groups=mesh['y1'=2,'y0'=2,'z1'=4,'z0'=2,'core'=2,'x'=4,'yl'=2] {'z1','z0','x','..., dimensions={0} | all-to-all | bytes 655360 | tf_op jit(solution)/shard_map/all_to_all | solution.py:307
  87.8 1.1 %combine.1 = (bf16[2,8192]{1,0:T(2,128)(2,1)}, f32[8,16]{1,0:T(8,128)}) custom-call(s32[640,128]{1,0:T(8,128)S(1)} %bitcast.8), custom_call_target="tpu_custom_call" | custom-call | tf_op jit(solution)/shard_map/combine/pallas_call | solution.py:270
  (1 shorter events, 0.0 us)
Async XLA Ops:
  0.6 0.9 %copy-start = (bf16[2,496,128]{2,1,0:T(8,128)(2,1)S(1)}, bf16[2,496,128]{2,1,0:T(8,128)(2,1)}, u32[]{:S(2)}) copy-start(bf16[2,496,128]{2,1,0:T(8,128)(2,1)} %cache_ref.1) | copy-start | bytes 761860
  1.6 0.7 copy-start.2
  2.3 20.8 %copy-start.1 = (bf16[2,8192]{1,0:T(2,128)(2,1)S(1)}, bf16[2,8192]{1,0:T(2,128)(2,1)}, u32[]{:S(2)}) copy-start(bf16[2,8192]{1,0:T(2,128)(2,1)} %q_ref.1) | copy-start | bytes 98308
  2.3 18.7 %collective-permute-start = (bf16[2,512,128]{2,1,0:T(8,128)(2,1)S(1)}, bf16[2,512,128]{2,1,0:T(8,128)(2,1)S(1)}, u32[]{:S(2)}, u32[]{:S(2)}) collective-permute-start(bf16[2,512,128]{2,1,0:T(8,128)(2,1)S(1)} %join.1.refs_0_), channel_id=1, source_target_pairs={{0,128},{8,392},{128,256},{136,8},{256,384},{264,136},{384,0},{392... | collective-permute-start | bytes 786440 | tf_op jit(solution)/shard_map/ppermute | solution.py:290
  8.0 13.0 %collective-permute-start.3 = (bf16[2,512,128]{2,1,0:T(8,128)(2,1)S(1)}, bf16[2,512,128]{2,1,0:T(8,128)(2,1)S(1)}, u32[]{:S(2)}, u32[]{:S(2)}) collective-permute-start(bf16[2,512,128]{2,1,0:T(8,128)(2,1)S(1)} %join.1.refs_0_), channel_id=1, source_target_pairs={{0,384},{8,136},{128,0},{136,264},{256,128},{264,392},{384,256},{3... | collective-permute-start | bytes 786440 | tf_op jit(solution)/shard_map/ppermute | solution.py:291
  21.1 34.5 %collective-permute-start.4 = (bf16[3,2,512,128]{3,2,1,0:T(8,128)(2,1)S(1)}, bf16[3,2,512,128]{3,2,1,0:T(8,128)(2,1)S(1)}, u32[]{:S(2)}, u32[]{:S(2)}) collective-permute-start(bf16[3,2,512,128]{3,2,1,0:T(8,128)(2,1)S(1)} %pair.1.refs_5_), channel_id=1, source_target_pairs={{0,8},{8,0},{1,9},{9,1},{2,10},{10,2},{3,11},{11,3},{4,12},{12,4},... | collective-permute-start | bytes 2359304 | tf_op jit(solution)/shard_map/ppermute | solution.py:298
  23.8 28.0 %copy-start.3 = (s32[1024]{0:T(1024)S(1)}, s32[1024]{0:T(1024)}, u32[]{:S(2)}) copy-start(s32[1024]{0:T(1024)} %ids_ref.1) | copy-start | bytes 12292
  23.9 28.0 %copy-start.4 = (s32[64]{0:T(128)S(1)}, s32[64]{0:T(128)}, u32[]{:S(2)}) copy-start(s32[64]{0:T(128)} %lens_ref.1) | copy-start | bytes 772
  23.9 29.1 %all-to-all-start = ((bf16[64,16,128]{2,1,0:T(8,128)(2,1)}), bf16[64,16,128]{2,1,0:T(8,128)(2,1)S(1)}, u32[]{:S(2)}, u32[]{:S(2)}) async-start(bf16[64,16,128]{2,1,0:T(8,128)(2,1)} %spread.1), calls=%async_computation | async-start | bytes 524288 | tf_op jit(solution)/shard_map/all_to_all | solution.py:294
  39.2 9.3 %collective-permute-start.1 = (bf16[2,512,128]{2,1,0:T(8,128)(2,1)S(1)}, bf16[2,512,128]{2,1,0:T(8,128)(2,1)S(1)}, u32[]{:S(2)}, u32[]{:S(2)}) collective-permute-start(bf16[2,512,128]{2,1,0:T(8,128)(2,1)S(1)} %collective-permute-done.refs_1_), channel_id=1, source_target_pairs={{0,128},{8,392},{128,256},{136,8},{256,384},{264,136},{384,0},{392... | collective-permute-start | bytes 786440 | tf_op jit(solution)/shard_map/ppermute | solution.py:292
  48.5 11.1 %collective-permute-start.2 = (bf16[2,512,128]{2,1,0:T(8,128)(2,1)S(1)}, bf16[2,512,128]{2,1,0:T(8,128)(2,1)S(1)}, u32[]{:S(2)}, u32[]{:S(2)}) collective-permute-start(bf16[2,512,128]{2,1,0:T(8,128)(2,1)S(1)} %collective-permute-done.1.refs_5_), channel_id=1, source_target_pairs={{0,8},{8,0},{1,9},{9,1},{2,10},{10,2},{3,11},{11,3},{4,12},{12,4},... | collective-permute-start | bytes 786440 | tf_op jit(solution)/shard_map/ppermute | solution.py:299

commit v6 on v5

--- a/solution.py
+++ b/solution.py
@@ -16,6 +16,7 @@
 CTX = ("y1", "y0", "z1", "z0", "core")
 TP = ("x", "yl")
 ROUTE = ("z1", "z0", "x", "yl")
+BACK = ("x", "yl", "z1", "z0")
 
 
 def prep_kernel(lens_ref, ids_ref, filled_ref, kseg_ref, qseg_ref, pick_ref):
@@ -196,7 +197,7 @@
                 lanes = slice(half * 128, (half + 1) * 128)
                 block = acc[:, lanes].T.astype(jnp.int32)
                 for t in range(8):
-                    to = ((part * (tile // 128) + half) * 8 + t) * SENT
+                    to = (t * 8 + part * (tile // 128) + half) * SENT
                     upper = block[t * 16 : t * 16 + 8, :]
                     lower = block[t * 16 + 8 : t * 16 + 16, :]
                     out_ref[to : to + 8, :] = (upper << 16) | (lower & 0xFFFF)
@@ -237,17 +238,17 @@
     lse = got_ref[pl.ds(8, 64, stride=SENT), :].astype(jnp.float32) * (1.0 / 65536.0)
     power = got_ref[pl.ds(9, 64, stride=SENT), :].astype(jnp.float32) - 15.0
     lse = lse.reshape(8, 8, 128)
-    peak = jnp.max(lse, axis=0)
-    w = jnp.exp(lse - peak[None])
-    denom = jnp.sum(w, axis=0)
-    w = (w / denom[None]).reshape(64, 128) * jnp.exp2(power)
+    peak = jnp.max(lse, axis=1)
+    w = jnp.exp(lse - peak[:, None])
+    denom = jnp.sum(w, axis=1)
+    w = (w / denom[:, None]).reshape(64, 128) * jnp.exp2(power)
     turned_ref[...] = jnp.concatenate([w, w], axis=0).T
     line_ref[...] = peak + jnp.log(denom)
     mine = turned_ref[pl.ds(pl.multiple_of(me * 16, 16), 16), :]
     for g in range(8):
         tops = bottoms = None
         for a in range(8):
-            at = a * 8 + g
+            at = g * 8 + a
             word = got_ref[at * SENT : at * SENT + 8, :]
             top = (word >> 16).astype(jnp.float32) * mine[:8, at : at + 1]
             bottom = ((word << 16) >> 16).astype(jnp.float32) * mine[8:, at : at + 1]
@@ -304,7 +305,7 @@
         flat = [j for entry in shards for j in (entry if isinstance(entry, tuple) else (entry,))]
         state = attend(flat, q, prepared, [chunk[j] for j in shards], state, final=final)
     sent = state.reshape(64, 1, SENT * 128)
-    got = lax.all_to_all(sent, ROUTE, split_axis=0, concat_axis=0, tiled=True)
+    got = lax.all_to_all(sent, BACK, split_axis=0, concat_axis=0, tiled=True)
     out, lse = combine(got.reshape(64 * SENT, 128))
     return out, lse.T
 

time: 89.4 us -> 89.4 us (level)
  the two profiles are of different devices: /device:TPU:16 before, /device:TPU:8 now
where the time goes in v6:
time: 89.4 us; the launch traced here: 88.9 us
  starting transfers between devices  34.7 us (39%)
  blocking collectives  25.5 us (29%)
  waiting for transfers between devices  15.7 us (18%)
  Pallas kernels  10.6 us (12%)
  local copies, waits for them, and re-layouts  1.65 us (2%)
    all_to_all x1, blocking collectives, shards_program(): got = lax.all_to_all(sent, BACK, split_axis=0, concat_axis=0, tiled=True)  25.5 us
    all_to_all x1, starting transfers between devices, shards_program(): q = lax.all_to_all(q, ROUTE, split_axis=0, concat_axis=0, tiled=True)  17.8 us
    ppermute x1, waiting for transfers between devices, shards_program(): two = lax.ppermute(one, ring, turn(1))  8 us
    pallas_call x4, Pallas kernels, attend(): pl.pallas_call(functools.partial(attend_kernel, tuple(shards), len(chunks...  7.8 us
    ppermute x1, waiting for transfers between devices, shards_program(): three = lax.ppermute(own, ring, turn(3))  5.23 us
    ppermute x1, starting transfers between devices, shards_program(): two = lax.ppermute(one, ring, turn(1))  5.07 us
    ppermute x1, starting transfers between devices, shards_program(): one = lax.ppermute(own, ring, turn(1))  4.5 us
    ppermute x1, starting transfers between devices, shards_program(): three = lax.ppermute(own, ring, turn(3))  3.45 us
  transfers between devices with their start and end apart: 6, of which 3 were waited for; matrix products, arithmetic and copies ran while one was open for 0% of the time, Pallas kernels for 9%

profile of v6, /device:TPU:8, one launch (start us, length us, event | category | flops | bytes accessed | tf_op | source)
XLA Modules:
  0.0 88.9 jit_solution(8738052070373816045)
XLA Ops:
  0.6 0.0 copy-start
  0.6 0.9 %copy-done = bf16[2,496,128]{2,1,0:T(8,128)(2,1)S(1)} copy-done((bf16[2,496,128]{2,1,0:T(8,128)(2,1)S(1)}, bf16[2,496,128]{2,1,0:T(8,128)(2,1)}, u32[]{:S(2)}) %copy-start) | copy-done | bytes 253976
  1.6 0.0 copy-start.2
  1.6 0.7 copy-done.2
  2.3 0.0 copy-start.1
  2.3 4.5 %collective-permute-start = (bf16[2,512,128]{2,1,0:T(8,128)(2,1)S(1)}, bf16[2,512,128]{2,1,0:T(8,128)(2,1)S(1)}, u32[]{:S(2)}, u32[]{:S(2)}) collective-permute-start(bf16[2,512,128]{2,1,0:T(8,128)(2,1)S(1)} %join.1.refs_0_), channel_id=1, source_target_pairs={{0,128},{8,392},{128,256},{136,8},{256,384},{264,136},{384,0},{392... | collective-permute-start | bytes 786440 | tf_op jit(solution)/shard_map/ppermute | solution.py:291
  6.8 3.5 %collective-permute-start.3 = (bf16[2,512,128]{2,1,0:T(8,128)(2,1)S(1)}, bf16[2,512,128]{2,1,0:T(8,128)(2,1)S(1)}, u32[]{:S(2)}, u32[]{:S(2)}) collective-permute-start(bf16[2,512,128]{2,1,0:T(8,128)(2,1)S(1)} %join.1.refs_0_), channel_id=1, source_target_pairs={{0,384},{8,136},{128,0},{136,264},{256,128},{264,392},{384,256},{3... | collective-permute-start | bytes 786440 | tf_op jit(solution)/shard_map/ppermute | solution.py:292
  10.3 2.5 %collective-permute-done.refs_1_ = bf16[2,512,128]{2,1,0:T(8,128)(2,1)S(1)} collective-permute-done((bf16[2,512,128]{2,1,0:T(8,128)(2,1)S(1)}, bf16[2,512,128]{2,1,0:T(8,128)(2,1)S(1)}, u32[]{:S(2)}, u32[]{:S(2)}) %collective-permute-start) | collective-permute-done | bytes 262176 | tf_op jit(solution)/shard_map/ppermute | solution.py:291
  12.8 5.2 %collective-permute-done.3.refs_2_ = bf16[2,512,128]{2,1,0:T(8,128)(2,1)S(1)} collective-permute-done((bf16[2,512,128]{2,1,0:T(8,128)(2,1)S(1)}, bf16[2,512,128]{2,1,0:T(8,128)(2,1)S(1)}, u32[]{:S(2)}, u32[]{:S(2)}) %collective-permute-start.3) | collective-permute-done | bytes 262176 | tf_op jit(solution)/shard_map/ppermute | solution.py:292
  18.0 0.1 pair.1.refs_5_
  18.1 1.9 %collective-permute-start.4 = (bf16[3,2,512,128]{3,2,1,0:T(8,128)(2,1)S(1)}, bf16[3,2,512,128]{3,2,1,0:T(8,128)(2,1)S(1)}, u32[]{:S(2)}, u32[]{:S(2)}) collective-permute-start(bf16[3,2,512,128]{3,2,1,0:T(8,128)(2,1)S(1)} %pair.1.refs_5_), channel_id=1, source_target_pairs={{0,8},{8,0},{1,9},{9,1},{2,10},{10,2},{3,11},{11,3},{4,12},{12,4},... | collective-permute-start | bytes 2359304 | tf_op jit(solution)/shard_map/ppermute | solution.py:299
  20.0 0.0 copy-done.1
  20.0 0.8 spread.1
  20.8 0.0 copy-start.3
  20.8 0.0 copy-start.4
  20.8 17.8 %all-to-all-start = ((bf16[64,16,128]{2,1,0:T(8,128)(2,1)}), bf16[64,16,128]{2,1,0:T(8,128)(2,1)S(1)}, u32[]{:S(2)}, u32[]{:S(2)}) async-start(bf16[64,16,128]{2,1,0:T(8,128)(2,1)} %spread.1), calls=%async_computation | async-start | bytes 524288 | tf_op jit(solution)/shard_map/all_to_all | solution.py:295
  38.6 5.1 %collective-permute-start.1 = (bf16[2,512,128]{2,1,0:T(8,128)(2,1)S(1)}, bf16[2,512,128]{2,1,0:T(8,128)(2,1)S(1)}, u32[]{:S(2)}, u32[]{:S(2)}) collective-permute-start(bf16[2,512,128]{2,1,0:T(8,128)(2,1)S(1)} %collective-permute-done.refs_1_), channel_id=1, source_target_pairs={{0,128},{8,392},{128,256},{136,8},{256,384},{264,136},{384,0},{392... | collective-permute-start | bytes 786440 | tf_op jit(solution)/shard_map/ppermute | solution.py:293
  43.7 8.0 %collective-permute-done.1.refs_5_ = bf16[2,512,128]{2,1,0:T(8,128)(2,1)S(1)} collective-permute-done((bf16[2,512,128]{2,1,0:T(8,128)(2,1)S(1)}, bf16[2,512,128]{2,1,0:T(8,128)(2,1)S(1)}, u32[]{:S(2)}, u32[]{:S(2)}) %collective-permute-start.1) | collective-permute-done | bytes 262176 | tf_op jit(solution)/shard_map/ppermute | solution.py:293
  51.7 1.9 %collective-permute-start.2 = (bf16[2,512,128]{2,1,0:T(8,128)(2,1)S(1)}, bf16[2,512,128]{2,1,0:T(8,128)(2,1)S(1)}, u32[]{:S(2)}, u32[]{:S(2)}) collective-permute-start(bf16[2,512,128]{2,1,0:T(8,128)(2,1)S(1)} %collective-permute-done.1.refs_5_), channel_id=1, source_target_pairs={{0,8},{8,0},{1,9},{9,1},{2,10},{10,2},{3,11},{11,3},{4,12},{12,4},... | collective-permute-start | bytes 786440 | tf_op jit(solution)/shard_map/ppermute | solution.py:300
  53.6 0.0 copy-done.3
  53.6 0.0 copy-done.4
  53.6 0.8 prep.1
  54.5 0.0 all-to-all-done
  54.5 2.6 %attend.4.refs_6_ = f32[136,1024]{1,0:T(8,128)S(1)} custom-call(bf16[1024,128]{1,0:T(8,128)(2,1)S(1)} %bitcast.4, s32[8,128]{1,0:T(8,128)S(1)} %get-tuple-element.8.refs_1_, s32[8,16,128]{2,1,0:T(8,128)S(1)} %get-tuple-element.9.refs_2_, s32[8,128]{1,0:T(8,128)S(1)} %get-tuple-element.10.refs_3_, bf16[1024,128]{1,0:T(8,128)(2,1)S(1)} %get-tuple-element.11.refs_4_, ...), custom_call_target="tpu_custom_call" | custom-call | flops 805306368 | bytes 1048576 | tf_op jit(solution)/shard_map/attend/pallas_call | solution.py:220
  57.1 0.0 collective-permute-done.4.refs_5_
  57.1 2.8 %attend.5.refs_6_ = f32[136,1024]{1,0:T(8,128)S(1)} custom-call(bf16[1024,128]{1,0:T(8,128)(2,1)S(1)} %bitcast.5, s32[8,128]{1,0:T(8,128)S(1)} %get-tuple-element.8.refs_1_, s32[8,16,128]{2,1,0:T(8,128)S(1)} %get-tuple-element.9.refs_2_, s32[8,128]{1,0:T(8,128)S(1)} %get-tuple-element.10.refs_3_, ...), custom_call_target="tpu_custom_call", output_to_operand_aliasing={{}: (6, {})} | custom-call | flops 805306368 | bytes 1048576 | tf_op jit(solution)/shard_map/attend/pallas_call | solution.py:220
  59.9 1.1 %attend.6.refs_6_ = f32[136,1024]{1,0:T(8,128)S(1)} custom-call(bf16[1024,128]{1,0:T(8,128)(2,1)S(1)} %bitcast.6, s32[8,128]{1,0:T(8,128)S(1)} %get-tuple-element.8.refs_1_, s32[8,16,128]{2,1,0:T(8,128)S(1)} %get-tuple-element.9.refs_2_, s32[8,128]{1,0:T(8,128)S(1)} %get-tuple-element.10.refs_3_, ...), custom_call_target="tpu_custom_call", output_to_operand_aliasing={{}: (6, {})} | custom-call | flops 268435456 | bytes 1048576 | tf_op jit(solution)/shard_map/attend/pallas_call | solution.py:220
  61.1 0.0 collective-permute-done.2.refs_5_
  61.1 1.2 %attend.7 = s32[640,128]{1,0:T(8,128)S(1)} custom-call(bf16[1024,128]{1,0:T(8,128)(2,1)S(1)} %bitcast.7, s32[8,128]{1,0:T(8,128)S(1)} %get-tuple-element.8.refs_1_, s32[8,16,128]{2,1,0:T(8,128)S(1)} %get-tuple-element.9.refs_2_, s32[8,128]{1,0:T(8,128)S(1)} %get-tuple-element.10.refs_3_, bf16[1024,128]{1,0:T(8,128)(2,1)S(1)} %get-tuple-element.11.refs_4_, ...), custom_call_target="tpu_custom_call" | custom-call | flops 268435456 | bytes 1048576 | tf_op jit(solution)/shard_map/attend/pallas_call | solution.py:220
  62.3 25.5 %all_to_all.10 = s32[64,1,1280]{2,1,0:T(1,128)S(1)} all-to-all(s32[64,1,1280]{2,1,0:T(1,128)S(1)} %bitcast.9), channel_id=1, replica_groups=mesh['y1'=2,'y0'=2,'z1'=4,'z0'=2,'core'=2,'x'=4,'yl'=2] {'x','yl','z1','..., dimensions={0} | all-to-all | bytes 655360 | tf_op jit(solution)/shard_map/all_to_all | solution.py:308
  87.8 1.1 %combine.1 = (bf16[2,8192]{1,0:T(2,128)(2,1)}, f32[8,16]{1,0:T(8,128)}) custom-call(s32[640,128]{1,0:T(8,128)S(1)} %bitcast.8), custom_call_target="tpu_custom_call" | custom-call | tf_op jit(solution)/shard_map/combine/pallas_call | solution.py:271
  (1 shorter events, 0.0 us)
Async XLA Ops:
  0.6 0.9 %copy-start = (bf16[2,496,128]{2,1,0:T(8,128)(2,1)S(1)}, bf16[2,496,128]{2,1,0:T(8,128)(2,1)}, u32[]{:S(2)}) copy-start(bf16[2,496,128]{2,1,0:T(8,128)(2,1)} %cache_ref.1) | copy-start | bytes 761860
  1.6 0.7 copy-start.2
  2.3 17.7 %copy-start.1 = (bf16[2,8192]{1,0:T(2,128)(2,1)S(1)}, bf16[2,8192]{1,0:T(2,128)(2,1)}, u32[]{:S(2)}) copy-start(bf16[2,8192]{1,0:T(2,128)(2,1)} %q_ref.1) | copy-start | bytes 98308
  2.3 10.5 %collective-permute-start = (bf16[2,512,128]{2,1,0:T(8,128)(2,1)S(1)}, bf16[2,512,128]{2,1,0:T(8,128)(2,1)S(1)}, u32[]{:S(2)}, u32[]{:S(2)}) collective-permute-start(bf16[2,512,128]{2,1,0:T(8,128)(2,1)S(1)} %join.1.refs_0_), channel_id=1, source_target_pairs={{0,128},{8,392},{128,256},{136,8},{256,384},{264,136},{384,0},{392... | collective-permute-start | bytes 786440 | tf_op jit(solution)/shard_map/ppermute | solution.py:291
  6.8 11.2 %collective-permute-start.3 = (bf16[2,512,128]{2,1,0:T(8,128)(2,1)S(1)}, bf16[2,512,128]{2,1,0:T(8,128)(2,1)S(1)}, u32[]{:S(2)}, u32[]{:S(2)}) collective-permute-start(bf16[2,512,128]{2,1,0:T(8,128)(2,1)S(1)} %join.1.refs_0_), channel_id=1, source_target_pairs={{0,384},{8,136},{128,0},{136,264},{256,128},{264,392},{384,256},{3... | collective-permute-start | bytes 786440 | tf_op jit(solution)/shard_map/ppermute | solution.py:292
  18.1 39.1 %collective-permute-start.4 = (bf16[3,2,512,128]{3,2,1,0:T(8,128)(2,1)S(1)}, bf16[3,2,512,128]{3,2,1,0:T(8,128)(2,1)S(1)}, u32[]{:S(2)}, u32[]{:S(2)}) collective-permute-start(bf16[3,2,512,128]{3,2,1,0:T(8,128)(2,1)S(1)} %pair.1.refs_5_), channel_id=1, source_target_pairs={{0,8},{8,0},{1,9},{9,1},{2,10},{10,2},{3,11},{11,3},{4,12},{12,4},... | collective-permute-start | bytes 2359304 | tf_op jit(solution)/shard_map/ppermute | solution.py:299
  20.8 32.8 %copy-start.3 = (s32[1024]{0:T(1024)S(1)}, s32[1024]{0:T(1024)}, u32[]{:S(2)}) copy-start(s32[1024]{0:T(1024)} %ids_ref.1) | copy-start | bytes 12292
  20.8 32.8 %copy-start.4 = (s32[64]{0:T(128)S(1)}, s32[64]{0:T(128)}, u32[]{:S(2)}) copy-start(s32[64]{0:T(128)} %lens_ref.1) | copy-start | bytes 772
  20.8 33.7 %all-to-all-start = ((bf16[64,16,128]{2,1,0:T(8,128)(2,1)}), bf16[64,16,128]{2,1,0:T(8,128)(2,1)S(1)}, u32[]{:S(2)}, u32[]{:S(2)}) async-start(bf16[64,16,128]{2,1,0:T(8,128)(2,1)} %spread.1), calls=%async_computation | async-start | bytes 524288 | tf_op jit(solution)/shard_map/all_to_all | solution.py:295
  38.6 13.1 %collective-permute-start.1 = (bf16[2,512,128]{2,1,0:T(8,128)(2,1)S(1)}, bf16[2,512,128]{2,1,0:T(8,128)(2,1)S(1)}, u32[]{:S(2)}, u32[]{:S(2)}) collective-permute-start(bf16[2,512,128]{2,1,0:T(8,128)(2,1)S(1)} %collective-permute-done.refs_1_), channel_id=1, source_target_pairs={{0,128},{8,392},{128,256},{136,8},{256,384},{264,136},{384,0},{392... | collective-permute-start | bytes 786440 | tf_op jit(solution)/shard_map/ppermute | solution.py:293
  51.7 9.4 %collective-permute-start.2 = (bf16[2,512,128]{2,1,0:T(8,128)(2,1)S(1)}, bf16[2,512,128]{2,1,0:T(8,128)(2,1)S(1)}, u32[]{:S(2)}, u32[]{:S(2)}) collective-permute-start(bf16[2,512,128]{2,1,0:T(8,128)(2,1)S(1)} %collective-permute-done.1.refs_5_), channel_id=1, source_target_pairs={{0,8},{8,0},{1,9},{9,1},{2,10},{10,2},{3,11},{11,3},{4,12},{12,4},... | collective-permute-start | bytes 786440 | tf_op jit(solution)/shard_map/ppermute | solution.py:300
